TPU v7x, 32 devices: a whole 2x2x4 slice. The times are simulated.
32 devices in a mesh: section: 2 (over x), tensor: 2 (over core), dp: 8 (over z, y).
Axes of the slice: x: 2, y: 2, z: 4, core: 2. Of those that a mesh axis runs over, the one named last changes fastest.
Arguments:
- inputs: bfloat16 [2, 1024, 2048], P(None, 'dp'), may hold values from -6 to 6
- cotangent: bfloat16 [2, 1024, 2048], P(None, 'dp'), may hold values from -6 to 6
- segments: int32 [2, 1024], P(None, 'dp'), may hold values from 0 to 3, never falling along the last dimension, each value on 1 to 512 neighbouring positions
- w_query: bfloat16 [2, 2048, 2048], P('section', 'dp', 'tensor'), may hold values from -0.125 to 0.125
- key_weight: bfloat16 [2, 2048, 1024], P('section', 'dp', 'tensor'), may hold values from -0.125 to 0.125
- value_weight: bfloat16 [2, 2048, 1024], P('section', 'dp', 'tensor'), may hold values from -0.125 to 0.125
- w_output: bfloat16 [2, 2048, 2048], P('section', 'dp', 'tensor'), may hold values from -0.5 to 0.5
- w_gate: bfloat16 [2, 2048, 6144], P('section', 'dp', 'tensor'), may hold values from -0.125 to 0.125
- w_up: bfloat16 [2, 2048, 6144], P('section', 'dp', 'tensor'), may hold values from -0.125 to 0.125
- w_down: bfloat16 [2, 2048, 6144], P('section', 'dp', 'tensor'), may hold values from -0.078125 to 0.078125
- attn_gain: bfloat16 [2, 2048], P('section', 'dp'), may hold values from 0.5 to 1.5
- mlp_gain: bfloat16 [2, 2048], P('section', 'dp'), may hold values from 0.5 to 1.5
- query_gain: bfloat16 [2, 128], P('section'), may hold values from 0.5 to 1.5
- key_gain: bfloat16 [2, 128], P('section'), may hold values from 0.5 to 1.5
Outputs:
- section_outputs: bfloat16 [2, 2, 1024, 2048], P('section', None, 'dp')
- input_grads: bfloat16 [2, 2, 1024, 2048], P('section', None, 'dp')
- grad_query: float32 [2, 2048, 2048], P('section', 'dp', 'tensor')
- grad_key: float32 [2, 2048, 1024], P('section', 'dp', 'tensor')
- grad_value: float32 [2, 2048, 1024], P('section', 'dp', 'tensor')
- grad_output: float32 [2, 2048, 2048], P('section', 'dp', 'tensor')
- grad_gate: float32 [2, 2048, 6144], P('section', 'dp', 'tensor')
- up_weight_grad: float32 [2, 2048, 6144], P('section', 'dp', 'tensor')
- grad_down: float32 [2, 2048, 6144], P('section', 'dp', 'tensor')
- grad_attn_gain: float32 [2, 2048], P('section', 'dp')
- grad_mlp_gain: float32 [2, 2048], P('section', 'dp')
- grad_query_gain: float32 [2, 128], P('section')
- grad_key_gain: float32 [2, 128], P('section')
Inputs may be any that keep to these rules, and one draw needn't show every extreme that they name: `segments`: segment numbers never fall along a micro-batch; each document holds 1 to 512 tokens of a micro-batch.
All inputs are finite; a program needn't handle non-finite values.
Results may differ from a plain program's by a relative error of at most 0.03.
Values may be sent and summed in bfloat16 or wider, within the bound.
No kernel may reach another device: no remote copies, remote signals or barrier semaphores. Data moves between devices by JAX's collectives and lax.ppermute only.
A program may use at most 320 MiB of HBM per device.

v0:
```python
from functools import partial

import jax
import jax.numpy as jnp
from jax import lax
from jax.sharding import PartitionSpec as P

EPSILON = 1e-06
MASKED = -1e30


def shifted(x, axis, by):
    count = lax.axis_size(axis)
    pairs = [(i, i + by) for i in range(count) if 0 <= i + by < count]
    return lax.ppermute(x, axis, pairs)


def as_sent(x):

    def short(part):
        return part.astype(jnp.bfloat16) if part.dtype == jnp.float32 else part

    return jax.tree.map(short, x)


def dot_plain(left, right):
    return jnp.dot(left, right, preferred_element_type=jnp.float32)


def dot_last(left, right):
    return lax.dot_general(
        left, right, (((1,), (1,)), ((), ())), preferred_element_type=jnp.float32
    )


def dot_first(left, right):
    return lax.dot_general(
        left, right, (((0,), (0,)), ((), ())), preferred_element_type=jnp.float32
    )


def rms_scale(values, norm_gain):
    return (
        values * lax.rsqrt(jnp.mean(values * values, axis=-1, keepdims=True) + EPSILON) * norm_gain
    )


def swiglu(gate_raw, up_raw):
    return jax.nn.silu(gate_raw) * up_raw


def rope_tables(positions, head_size):
    half_size = head_size // 2
    freqs = jnp.power(
        jnp.float32(1000000.0), -jnp.arange(half_size, dtype=jnp.float32) * 2.0 / head_size
    )
    angles = positions.astype(jnp.float32)[:, None] * freqs[None, :]
    angles = jnp.concatenate([angles, angles], axis=-1)
    return (jnp.cos(angles), jnp.sin(angles))


def rotate_norm(raw_proj, norm_gain, cosine, sine_table):
    head_size = norm_gain.shape[0]
    token_count = raw_proj.shape[0]
    heads = raw_proj.reshape(token_count, -1, head_size)
    normed = rms_scale(heads, norm_gain)
    half_size = head_size // 2
    turned = jnp.concatenate([-normed[..., half_size:], normed[..., :half_size]], axis=-1)
    rotated = normed * cosine[:, None, :] + turned * sine_table[:, None, :]
    return rotated.reshape(token_count, -1)


def scores_for(queries, keys_all, allowed, head_size):
    row_count = queries.shape[0]
    kv_heads = keys_all.shape[1] // head_size
    group_size = queries.shape[1] // keys_all.shape[1]
    query_heads = queries.reshape(row_count, kv_heads, group_size, head_size)
    key_heads = keys_all.reshape(keys_all.shape[0], kv_heads, head_size)
    scores = jnp.einsum(
        "bngd,snd->ngbs", query_heads, key_heads, preferred_element_type=jnp.float32
    ) * head_size ** (-0.5)
    return (jnp.where(allowed[None, None], scores, MASKED), query_heads, key_heads)


def attend(queries, keys_all, values_all, allowed, head_size):
    scores, query_heads, key_heads = scores_for(queries, keys_all, allowed, head_size)
    highest = jnp.max(scores, axis=-1, keepdims=True)
    weights = jnp.exp(scores - highest)
    total = jnp.sum(weights, axis=-1, keepdims=True)
    probs = (weights / total).astype(jnp.bfloat16)
    value_heads = values_all.reshape(key_heads.shape)
    mixed = jnp.einsum("ngbs,snd->bngd", probs, value_heads, preferred_element_type=jnp.float32)
    return (mixed.reshape(queries.shape[0], -1).astype(jnp.bfloat16), highest + jnp.log(total))


def attend_back(queries, keys_all, values_all, allowed, log_total, attn_grad, head_size):
    scores, query_heads, key_heads = scores_for(queries, keys_all, allowed, head_size)
    probs = jnp.exp(scores - log_total)
    value_heads = values_all.reshape(key_heads.shape)
    grad_heads = attn_grad.reshape(query_heads.shape)
    prob_grad = jnp.einsum(
        "bngd,snd->ngbs", grad_heads, value_heads, preferred_element_type=jnp.float32
    )
    delta = jnp.sum(probs * prob_grad, axis=-1, keepdims=True)
    score_grad = (probs * (prob_grad - delta)).astype(jnp.bfloat16)
    scale = head_size ** (-0.5)
    query_back = jnp.einsum(
        "ngbs,snd->bngd", score_grad, key_heads, preferred_element_type=jnp.float32
    )
    key_back = jnp.einsum(
        "ngbs,bngd->snd", score_grad, query_heads, preferred_element_type=jnp.float32
    )
    value_back = jnp.einsum(
        "ngbs,bngd->snd", probs.astype(jnp.bfloat16), grad_heads, preferred_element_type=jnp.float32
    )
    key_count = keys_all.shape[0]
    return (
        query_back.reshape(queries.shape[0], -1) * scale,
        key_back.reshape(key_count, -1) * scale,
        value_back.reshape(key_count, -1),
    )


def per_device(
    inputs,
    cotangent,
    segments,
    w_query,
    key_weight,
    value_weight,
    w_output,
    w_gate,
    w_up,
    w_down,
    attn_gain,
    mlp_gain,
    query_gain,
    key_gain,
):
    section_first = lax.axis_index("section") == 0
    gathered = (
        lax.all_gather(w_query[0], "dp", axis=0, tiled=True),
        lax.all_gather(key_weight[0], "dp", axis=0, tiled=True),
        lax.all_gather(value_weight[0], "dp", axis=0, tiled=True),
        lax.all_gather(w_output[0], "dp", axis=0, tiled=True),
        lax.all_gather(w_gate[0], "dp", axis=0, tiled=True),
        lax.all_gather(w_up[0], "dp", axis=0, tiled=True),
        lax.all_gather(w_down[0], "dp", axis=0, tiled=True),
        lax.all_gather(attn_gain[0], "dp", axis=0, tiled=True),
        lax.all_gather(mlp_gain[0], "dp", axis=0, tiled=True),
    )
    w_q, w_k, w_v, w_o, w_g, w_u, w_d = gathered[:7]
    gain_attn = gathered[7].astype(jnp.float32)
    gain_mlp = gathered[8].astype(jnp.float32)
    gain_q = query_gain[0].astype(jnp.float32)
    gain_k = key_gain[0].astype(jnp.float32)
    head_size = gain_q.shape[0]
    doc_table = lax.all_gather(segments, "dp", axis=1, tiled=True)
    batch_count, row_count, model_width = inputs.shape
    token_count = doc_table.shape[1]
    positions = lax.axis_index("dp") * row_count + jnp.arange(row_count, dtype=jnp.int32)
    key_pos = jnp.arange(token_count, dtype=jnp.int32)
    cosine, sine_table = rope_tables(positions, head_size)
    rope_query = partial(rotate_norm, cosine=cosine, sine_table=sine_table)
    arrived = jnp.zeros((row_count, model_width), jnp.bfloat16)
    stored_steps, outgoing_steps = ([], [])
    for step_index in range(batch_count + 1):
        early = min(step_index, batch_count - 1)
        late = max(step_index - 1, 0)
        layer_in = jnp.where(
            section_first, inputs[early].astype(jnp.float32), arrived.astype(jnp.float32)
        )
        own_segs = jnp.where(section_first, segments[early], segments[late])
        doc_row = jnp.where(section_first, doc_table[early], doc_table[late])
        forward_normed = rms_scale(layer_in, gain_attn).astype(jnp.bfloat16)
        forward_queries = dot_plain(forward_normed, w_q)
        forward_key_raw = dot_plain(forward_normed, w_k)
        forward_value_raw = dot_plain(forward_normed, w_v).astype(jnp.bfloat16)
        forward_query_rot = rope_query(forward_queries, gain_q).astype(jnp.bfloat16)
        forward_key_rot = rope_query(forward_key_raw, gain_k).astype(jnp.bfloat16)
        forward_keys_all = lax.all_gather(forward_key_rot, "dp", axis=0, tiled=True)
        forward_values_all = lax.all_gather(forward_value_raw, "dp", axis=0, tiled=True)
        forward_allowed = (key_pos[None, :] <= positions[:, None]) & (
            own_segs[:, None] == doc_row[None, :]
        )
        forward_attn, forward_log_total = attend(
            forward_query_rot, forward_keys_all, forward_values_all, forward_allowed, head_size
        )
        forward_mixed = layer_in + lax.psum(dot_last(forward_attn, w_o), "tensor")
        forward_normed_mlp = rms_scale(forward_mixed, gain_mlp).astype(jnp.bfloat16)
        forward_gate_raw = dot_plain(forward_normed_mlp, w_g)
        forward_up_raw = dot_plain(forward_normed_mlp, w_u)
        forward_activated = swiglu(forward_gate_raw, forward_up_raw).astype(jnp.bfloat16)
        layer_out = forward_mixed + lax.psum(dot_last(forward_activated, w_d), "tensor")
        forward_stored = (
            layer_in,
            forward_normed,
            forward_queries,
            forward_key_raw,
            forward_query_rot,
            forward_key_rot,
            forward_value_raw,
            forward_attn,
            forward_log_total,
            forward_mixed,
            forward_normed_mlp,
            forward_gate_raw,
            forward_up_raw,
            forward_activated,
            forward_allowed,
        )
        layer_out, stored = (layer_out, forward_stored)
        outgoing = layer_out.astype(jnp.bfloat16)
        stored_steps.append(stored)
        outgoing_steps.append(outgoing)
        if step_index < batch_count:
            arrived = shifted(outgoing, "section", 1)
    section_out = jnp.stack(
        [
            jnp.where(section_first, outgoing_steps[batch_index], outgoing_steps[batch_index + 1])
            for batch_index in range(batch_count)
        ]
    )
    back_arrived = jnp.zeros((row_count, model_width), jnp.bfloat16)
    grad_steps = []
    totals = None
    norm_totals = None
    for step_index in range(batch_count + 1):
        early_batch = min(batch_count - step_index, batch_count - 1)
        late_batch = max(batch_count - 1 - step_index, 0)
        stored = jax.tree.map(
            lambda a, b: jnp.where(section_first, a, b),
            stored_steps[early_batch],
            stored_steps[late_batch + 1],
        )
        valid = jnp.where(
            section_first,
            jnp.float32(1.0 if step_index >= 1 else 0.0),
            jnp.float32(1.0 if step_index < batch_count else 0.0),
        )
        grad_out = (
            jnp.where(
                section_first,
                back_arrived.astype(jnp.float32),
                cotangent[late_batch].astype(jnp.float32),
            )
            * valid
        )
        (
            backward_layer_in,
            normed,
            queries,
            key_raw,
            query_rot,
            key_rot,
            value_raw,
            attn,
            log_total,
            mixed,
            normed_mlp,
            gate_raw,
            up_raw,
            activated,
            allowed,
        ) = stored[:15]
        keys_all = lax.all_gather(key_rot, "dp", axis=0, tiled=True)
        values_all = lax.all_gather(value_raw, "dp", axis=0, tiled=True)
        mlp_grad = grad_out.astype(jnp.bfloat16)
        act_grad = dot_plain(mlp_grad, w_d)
        grad_wd = dot_first(mlp_grad, activated)
        unused, swiglu_back = jax.vjp(swiglu, gate_raw, up_raw)
        gate_grad, up_grad = swiglu_back(act_grad)
        gate_grad = gate_grad.astype(jnp.bfloat16)
        up_grad = up_grad.astype(jnp.bfloat16)
        grad_wg = dot_first(normed_mlp, gate_grad)
        grad_wu = dot_first(normed_mlp, up_grad)
        normed_mlp_grad = lax.psum(
            (dot_last(gate_grad, w_g) + dot_last(up_grad, w_u)).astype(jnp.bfloat16), "tensor"
        ).astype(jnp.float32)
        unused, mlp_norm_back = jax.vjp(rms_scale, mixed, gain_mlp)
        mixed_part, grad_gain_mlp = mlp_norm_back(normed_mlp_grad)
        mixed_grad = grad_out + mixed_part
        branch_low = mixed_grad.astype(jnp.bfloat16)
        attn_grad = dot_plain(branch_low, w_o).astype(jnp.bfloat16)
        grad_wo = dot_first(branch_low, attn)
        query_back, key_back, value_back = attend_back(
            query_rot, keys_all, values_all, allowed, log_total, attn_grad, head_size
        )
        backward_key_total = lax.psum_scatter(
            key_back.astype(jnp.bfloat16), "dp", scatter_dimension=0, tiled=True
        ).astype(jnp.float32)
        value_total = lax.psum_scatter(
            value_back.astype(jnp.bfloat16), "dp", scatter_dimension=0, tiled=True
        )
        unused, key_rope_back = jax.vjp(rope_query, key_raw, gain_k)
        key_gradient, grad_gain_k = key_rope_back(backward_key_total)
        key_gradient = key_gradient.astype(jnp.bfloat16)
        unused, query_rope_back = jax.vjp(rope_query, queries, gain_q)
        query_grad, grad_gain_q = query_rope_back(query_back)
        query_grad = query_grad.astype(jnp.bfloat16)
        grad_wq = dot_first(normed, query_grad)
        grad_wk = dot_first(normed, key_gradient)
        grad_wv = dot_first(normed, value_total)
        normed_grad = lax.psum(
            (
                dot_last(query_grad, w_q) + dot_last(key_gradient, w_k) + dot_last(value_total, w_v)
            ).astype(jnp.bfloat16),
            "tensor",
        ).astype(jnp.float32)
        unused, attn_norm_back = jax.vjp(rms_scale, backward_layer_in, gain_attn)
        input_part, grad_gain_attn = attn_norm_back(normed_grad)
        weight_part = (
            grad_wq,
            grad_wk,
            grad_wv,
            grad_wo,
            grad_wg,
            grad_wu,
            grad_wd,
            grad_gain_attn,
            grad_gain_mlp,
        )
        input_grad, weight_part, norm_part = (
            mixed_grad + input_part,
            weight_part,
            (grad_gain_q, grad_gain_k),
        )
        outgoing = input_grad.astype(jnp.bfloat16)
        grad_steps.append(outgoing)
        if step_index < batch_count:
            back_arrived = shifted(outgoing, "section", -1)
        totals = (
            weight_part if totals is None else tuple((a + b for a, b in zip(totals, weight_part)))
        )
        norm_totals = (
            norm_part
            if norm_totals is None
            else tuple((a + b for a, b in zip(norm_totals, norm_part)))
        )
    shards = jax.tree.map(
        lambda part: part.astype(jnp.float32),
        lax.psum_scatter(as_sent(totals), "dp", scatter_dimension=0, tiled=True),
    )
    query_total, key_total = lax.psum(norm_totals, ("tensor", "dp"))
    input_grads = jnp.stack(
        [
            jnp.where(
                section_first,
                grad_steps[batch_count - batch_index],
                grad_steps[batch_count - 1 - batch_index],
            )
            for batch_index in range(batch_count)
        ]
    )
    return (
        (section_out[None], input_grads[None])
        + tuple((member[None] for member in shards))
        + (query_total[None], key_total[None])
    )


def solution(mesh):
    return jax.shard_map(
        per_device,
        mesh=mesh,
        in_specs=(
            P(None, "dp", None),
            P(None, "dp", None),
            P(None, "dp"),
            P("section", "dp", "tensor"),
            P("section", "dp", "tensor"),
            P("section", "dp", "tensor"),
            P("section", "dp", "tensor"),
            P("section", "dp", "tensor"),
            P("section", "dp", "tensor"),
            P("section", "dp", "tensor"),
            P("section", "dp"),
            P("section", "dp"),
            P("section", None),
            P("section", None),
        ),
        out_specs=(
            P("section", None, "dp", None),
            P("section", None, "dp", None),
            P("section", "dp", "tensor"),
            P("section", "dp", "tensor"),
            P("section", "dp", "tensor"),
            P("section", "dp", "tensor"),
            P("section", "dp", "tensor"),
            P("section", "dp", "tensor"),
            P("section", "dp", "tensor"),
            P("section", "dp"),
            P("section", "dp"),
            P("section", None),
            P("section", None),
        ),
        check_vma=False,
    )
```

profile of v0, /device:TPU:0, one launch (start us, length us, event | category | flops | bytes accessed | tf_op | source)
XLA Modules:
  0.0 3046.1 jit_solution(11934265292568928759)
XLA Ops:
  34.9 27.1 all-gather.47.cloned.1.call-done
  65.0 46.8 %all-gather.49.cloned.1.call-done = bf16[1,2048,512]{2,1,0:T(8,128)(2,1)} async-done(((bf16[1,256,512]{2,1,0:T(8,128)(2,1)}), bf16[1,2048,512]{2,1,0:T(8,128)(2,1)}) %all-gather.49.cloned.1.call-update) | async-done | bytes 2097168 | tf_op jit(solution)/shard_map/all_gather | solution.py:143
  155.1 38.7 %all-gather.29.cloned.1.call-done = bf16[1024,512]{1,0:T(8,128)(2,1)} async-done(((bf16[128,512]{1,0:T(8,128)(2,1)}), bf16[1024,512]{1,0:T(8,128)(2,1)}) %all-gather.29.cloned.1.call-update) | async-done | bytes 1048592 | tf_op jit(solution)/shard_map/all_gather | solution.py:181
  195.9 71.4 %all-gather.51.cloned.1.call-done = bf16[1,2048,1024]{2,1,0:T(8,128)(2,1)} async-done(((bf16[1,256,1024]{2,1,0:T(8,128)(2,1)}), bf16[1,2048,1024]{2,1,0:T(8,128)(2,1)}) %all-gather.51.cloned.1.call-update) | async-done | bytes 4194320 | tf_op jit(solution)/shard_map/all_gather | solution.py:142
  277.6 63.0 %all-gather.53.cloned.1.call-done = bf16[1,2048,1024]{2,1,0:T(8,128)(2,1)} async-done(((bf16[1,256,1024]{2,1,0:T(8,128)(2,1)}), bf16[1,2048,1024]{2,1,0:T(8,128)(2,1)}) %all-gather.53.cloned.1.call-update) | async-done | bytes 4194320 | tf_op jit(solution)/shard_map/all_gather | solution.py:145
  368.9 174.1 %all-gather.55.cloned.1.call-done = bf16[1,2048,3072]{2,1,0:T(8,128)(2,1)} async-done(((bf16[1,256,3072]{2,1,0:T(8,128)(2,1)}), bf16[1,2048,3072]{2,1,0:T(8,128)(2,1)}) %all-gather.55.cloned.1.call-update) | async-done | bytes 12582928 | tf_op jit(solution)/shard_map/all_gather | solution.py:146
  550.5 169.0 %all-gather.57.cloned.1.call-done = bf16[1,2048,3072]{2,1,0:T(8,128)(2,1)} async-done(((bf16[1,256,3072]{2,1,0:T(8,128)(2,1)}), bf16[1,2048,3072]{2,1,0:T(8,128)(2,1)}) %all-gather.57.cloned.1.call-update) | async-done | bytes 12582928 | tf_op jit(solution)/shard_map/all_gather | solution.py:147
  727.9 167.9 %all-gather.59.cloned.1.call-done = bf16[1,2048,3072]{2,1,0:T(8,128)(2,1)} async-done(((bf16[1,256,3072]{2,1,0:T(8,128)(2,1)}), bf16[1,2048,3072]{2,1,0:T(8,128)(2,1)}) %all-gather.59.cloned.1.call-update) | async-done | bytes 12582928 | tf_op jit(solution)/shard_map/all_gather | solution.py:148
  996.7 33.9 %all-gather.31.cloned.1.call-done = bf16[1024,512]{1,0:T(8,128)(2,1)} async-done(((bf16[128,512]{1,0:T(8,128)(2,1)}), bf16[1024,512]{1,0:T(8,128)(2,1)}) %all-gather.31.cloned.1.call-update) | async-done | bytes 1048592 | tf_op jit(solution)/shard_map/all_gather | solution.py:182
  1171.6 38.7 %all-gather.37.cloned.1.call-done = bf16[1024,512]{1,0:T(8,128)(2,1)} async-done(((bf16[128,512]{1,0:T(8,128)(2,1)}), bf16[1024,512]{1,0:T(8,128)(2,1)}) %all-gather.37.cloned.1.call-update) | async-done | bytes 1048592 | tf_op jit(solution)/shard_map/all_gather | solution.py:181
  1256.1 36.4 %all-gather.41.cloned.1.call-done = bf16[1024,512]{1,0:T(8,128)(2,1)} async-done(((bf16[128,512]{1,0:T(8,128)(2,1)}), bf16[1024,512]{1,0:T(8,128)(2,1)}) %all-gather.41.cloned.1.call-update) | async-done | bytes 1048592 | tf_op jit(solution)/shard_map/all_gather | solution.py:267
  1410.6 40.7 %reduce-scatter.40.cloned.1.call-done = bf16[128,512]{1,0:T(8,128)(2,1)} async-done(((bf16[1024,512]{1,0:T(8,128)(2,1)}), bf16[128,512]{1,0:T(8,128)(2,1)}) %reduce-scatter.40.cloned.1.call-update) | async-done | bytes 131088
  1460.6 57.9 %reduce-scatter.42.cloned.1.call-done = bf16[128,512]{1,0:T(8,128)(2,1)} async-done(((bf16[1024,512]{1,0:T(8,128)(2,1)}), bf16[128,512]{1,0:T(8,128)(2,1)}) %reduce-scatter.42.cloned.1.call-update) | async-done | bytes 131088
  1636.3 51.8 %reduce-scatter.44.cloned.1.call-done = bf16[128,512]{1,0:T(8,128)(2,1)} async-done(((bf16[1024,512]{1,0:T(8,128)(2,1)}), bf16[128,512]{1,0:T(8,128)(2,1)}) %reduce-scatter.44.cloned.1.call-update) | async-done | bytes 131088
  1691.0 64.1 %reduce-scatter.46.cloned.1.call-done = bf16[128,512]{1,0:T(8,128)(2,1)} async-done(((bf16[1024,512]{1,0:T(8,128)(2,1)}), bf16[128,512]{1,0:T(8,128)(2,1)}) %reduce-scatter.46.cloned.1.call-update) | async-done | bytes 131088
  1788.0 35.8 %all-gather.43.cloned.1.call-done = bf16[1024,512]{1,0:T(8,128)(2,1)} async-done(((bf16[128,512]{1,0:T(8,128)(2,1)}), bf16[1024,512]{1,0:T(8,128)(2,1)}) %all-gather.43.cloned.1.call-update) | async-done | bytes 1048592 | tf_op jit(solution)/shard_map/all_gather | solution.py:266
  1975.1 57.8 %reduce-scatter.50.cloned.1.call-done = bf16[128,512]{1,0:T(8,128)(2,1)} async-done(((bf16[1024,512]{1,0:T(8,128)(2,1)}), bf16[128,512]{1,0:T(8,128)(2,1)}) %reduce-scatter.50.cloned.1.call-update) | async-done | bytes 131088
  2172.8 22.8 add_convert_fusion
  2201.6 31.0 %all-reduce.14 = (f32[1,128]{1,0:T(1,128)}, f32[1,128]{1,0:T(1,128)}) all-reduce(f32[1,128]{1,0:T(1,128)S(1)} %add_bitcast_fusion.1, f32[1,128]{1,0:T(1,128)S(1)} %add_bitcast_fusion), channel_id=1, replica_groups=mesh['section'=2,'tensor'=2,'dp'=8] {'tensor','dp'}, use_global_device_ids=true, to_apply=%region_77.78 | all-reduce | flops 256 | bytes 2048 | tf_op jit(solution)/shard_map/psum | solution.py:344
  2261.9 51.4 %reduce-scatter.26.cloned.1.call-done = bf16[256,1024]{1,0:T(8,128)(2,1)} async-done(((bf16[2048,1024]{1,0:T(8,128)(2,1)}), bf16[256,1024]{1,0:T(8,128)(2,1)}) %reduce-scatter.26.cloned.1.call-update) | async-done | bytes 524304 | tf_op jit(solution)/shard_map/reduce_scatter | solution.py:342
  2315.4 89.3 %reduce-scatter.32.cloned.1.call-done = bf16[256,1024]{1,0:T(8,128)(2,1)} async-done(((bf16[2048,1024]{1,0:T(8,128)(2,1)}), bf16[256,1024]{1,0:T(8,128)(2,1)}) %reduce-scatter.32.cloned.1.call-update) | async-done | bytes 524304 | tf_op jit(solution)/shard_map/reduce_scatter | solution.py:342
  2406.9 208.6 %reduce-scatter.34.cloned.1.call-done = bf16[256,3072]{1,0:T(8,128)(2,1)} async-done(((bf16[2048,3072]{1,0:T(8,128)(2,1)}), bf16[256,3072]{1,0:T(8,128)(2,1)}) %reduce-scatter.34.cloned.1.call-update) | async-done | bytes 1572880 | tf_op jit(solution)/shard_map/reduce_scatter | solution.py:342
  2618.9 206.7 %reduce-scatter.36.cloned.1.call-done = bf16[256,3072]{1,0:T(8,128)(2,1)} async-done(((bf16[2048,3072]{1,0:T(8,128)(2,1)}), bf16[256,3072]{1,0:T(8,128)(2,1)}) %reduce-scatter.36.cloned.1.call-update) | async-done | bytes 1572880 | tf_op jit(solution)/shard_map/reduce_scatter | solution.py:342
  2829.0 206.7 %reduce-scatter.38.cloned.1.call-done = bf16[256,3072]{1,0:T(8,128)(2,1)} async-done(((bf16[2048,3072]{1,0:T(8,128)(2,1)}), bf16[256,3072]{1,0:T(8,128)(2,1)}) %reduce-scatter.38.cloned.1.call-update) | async-done | bytes 1572880 | tf_op jit(solution)/shard_map/reduce_scatter | solution.py:342
  (805 shorter events, 1036.4 us)
Async XLA Ops:
  8.7 144.1 %all-gather.27.cloned.1.call-start = ((), (), s32[]{:S(2)}) async-start(), calls=%async_computation.13 | async-start | bytes 1179648 | tf_op jit(solution)/shard_map/all_gather | solution.py:182
  115.9 151.4 %all-gather.51.cloned.1.call-start = ((), (), s32[]{:S(2)}) async-start(), calls=%async_computation.44 | async-start | bytes 4718592 | tf_op jit(solution)/shard_map/all_gather | solution.py:142
  116.5 224.1 %all-gather.53.cloned.1.call-start = ((), (), s32[]{:S(2)}) async-start(), calls=%async_computation.45 | async-start | bytes 4718592 | tf_op jit(solution)/shard_map/all_gather | solution.py:145
  117.1 248.8 %all-reduce.29.cloned.1.call-start = ((), (), s32[]{:S(2)}) async-start(), calls=%async_computation.15 | async-start | bytes 2097152 | tf_op jit(solution)/shard_map/psum | solution.py:189
  345.3 197.6 %all-gather.55.cloned.1.call-start = ((), (), s32[]{:S(2)}) async-start(), calls=%async_computation.46 | async-start | bytes 14155776 | tf_op jit(solution)/shard_map/all_gather | solution.py:146
  346.1 373.4 %all-gather.57.cloned.1.call-start = ((), (), s32[]{:S(2)}) async-start(), calls=%async_computation.47 | async-start | bytes 14155776 | tf_op jit(solution)/shard_map/all_gather | solution.py:147
  346.8 549.0 %all-gather.59.cloned.1.call-start = ((), (), s32[]{:S(2)}) async-start(), calls=%async_computation.48 | async-start | bytes 14155776 | tf_op jit(solution)/shard_map/all_gather | solution.py:148
  347.4 576.3 %all-reduce.31.cloned.1.call-start = ((), (), s32[]{:S(2)}) async-start(), calls=%async_computation.16 | async-start | bytes 2097152 | tf_op jit(solution)/shard_map/psum | solution.py:194
  1134.9 157.6 %all-gather.41.cloned.1.call-start = ((), (), s32[]{:S(2)}) async-start(), calls=%async_computation.27 | async-start | bytes 1179648 | tf_op jit(solution)/shard_map/all_gather | solution.py:267
  1148.7 164.7 %all-reduce.37.cloned.1.call-start = ((), (), s32[]{:S(2)}) async-start(), calls=%async_computation.23 | async-start | bytes 2097152 | tf_op jit(solution)/shard_map/psum | solution.py:189
  1220.5 148.0 %all-reduce.41.cloned.1.call-start = ((), (), s32[]{:S(2)}) async-start(), calls=%async_computation.25 | async-start | bytes 1048576 | tf_op jit(solution)/shard_map/psum | solution.py:277
  1385.7 132.7 %reduce-scatter.42.cloned.1.call-start = ((), (), s32[]{:S(2)}) async-start(), calls=%async_computation.50 | async-start | bytes 1179648
  1403.8 139.8 %all-reduce.43.cloned.1.call-start = ((), (), s32[]{:S(2)}) async-start(), calls=%async_computation.28 | async-start | bytes 1048576 | tf_op jit(solution)/shard_map/psum | solution.py:304
  1631.6 148.6 %all-reduce.47.cloned.1.call-start = ((), (), s32[]{:S(2)}) async-start(), calls=%async_computation.30 | async-start | bytes 1048576 | tf_op jit(solution)/shard_map/psum | solution.py:304
  1900.2 132.7 %reduce-scatter.50.cloned.1.call-start = ((), (), s32[]{:S(2)}) async-start(), calls=%async_computation.54 | async-start | bytes 1179648
  1906.9 290.6 %all-reduce.39.cloned.1.call-start = ((), (), s32[]{:S(2)}) async-start(), calls=%async_computation.24 | async-start | bytes 2097152 | tf_op jit(solution)/shard_map/psum | solution.py:194
  1926.4 306.2 %all-reduce.51.cloned.1.call-start = ((), (), s32[]{:S(2)}) async-start(), calls=%async_computation.34 | async-start | bytes 1048576 | tf_op jit(solution)/shard_map/psum | solution.py:304
  2039.6 218.6 %reduce-scatter.28.cloned.1.call-start = ((), (), s32[]{:S(2)}) async-start(), calls=%async_computation.36 | async-start | bytes 2359296 | tf_op jit(solution)/shard_map/reduce_scatter | solution.py:342
  2044.5 215.6 %reduce-scatter.30.cloned.1.call-start = ((), (), s32[]{:S(2)}) async-start(), calls=%async_computation.37 | async-start | bytes 2359296 | tf_op jit(solution)/shard_map/reduce_scatter | solution.py:342
  2048.2 265.1 %reduce-scatter.26.cloned.1.call-start = ((), (), s32[]{:S(2)}) async-start(), calls=%async_computation.35 | async-start | bytes 4718592 | tf_op jit(solution)/shard_map/reduce_scatter | solution.py:342
  2054.4 350.4 %reduce-scatter.32.cloned.1.call-start = ((), (), s32[]{:S(2)}) async-start(), calls=%async_computation.38 | async-start | bytes 4718592 | tf_op jit(solution)/shard_map/reduce_scatter | solution.py:342
  2061.8 553.6 %reduce-scatter.34.cloned.1.call-start = ((), (), s32[]{:S(2)}) async-start(), calls=%async_computation.39 | async-start | bytes 14155776 | tf_op jit(solution)/shard_map/reduce_scatter | solution.py:342
  2106.2 719.4 %reduce-scatter.36.cloned.1.call-start = ((), (), s32[]{:S(2)}) async-start(), calls=%async_computation.40 | async-start | bytes 14155776 | tf_op jit(solution)/shard_map/reduce_scatter | solution.py:342
  2150.5 885.2 %reduce-scatter.38.cloned.1.call-start = ((), (), s32[]{:S(2)}) async-start(), calls=%async_computation.41 | async-start | bytes 14155776 | tf_op jit(solution)/shard_map/reduce_scatter | solution.py:342
  (200 other events, 6141.9 us)
Sparse Core Ops, SparseCore 0:
  10.1 51.8 all-gather.46
  64.1 47.6 all-gather.48
  195.8 71.4 all-gather.50
  269.3 71.3 all-gather.52
  365.7 177.2 all-gather.54
  545.2 174.2 all-gather.56
  721.5 174.2 all-gather.58
  947.3 42.1 all-gather.32
  1127.5 41.8 all-gather.34
  1385.8 65.4 reduce-scatter.39
  1455.3 63.1 reduce-scatter.41
  1622.7 65.4 reduce-scatter.43
  1692.0 63.1 reduce-scatter.45
  1782.3 41.4 all-gather.42
  1826.0 38.9 all-gather.44
  1900.3 65.4 reduce-scatter.47
  1969.6 63.1 reduce-scatter.49
  2080.4 69.4 reduce-scatter.27
  2153.9 67.9 reduce-scatter.29
  2225.5 87.7 reduce-scatter.25
  2316.8 87.9 reduce-scatter.31
  2408.3 207.0 reduce-scatter.33
  2619.0 206.5 reduce-scatter.35
  2829.2 206.5 reduce-scatter.37
  (18 shorter events, 453.5 us)
where the time goes:
time: 3060 us; the launch traced here: 3050 us
  waiting for transfers between devices  2250 us (74%)
  matrix products  412 us (13%)
  other arithmetic  132 us (4%)
  blocking collectives  110 us (4%)
  local copies, waits for them, and re-layouts  98.5 us (3%)
    reduce_scatter x7, waiting for transfers between devices, per_device(): lax.psum_scatter(as_sent(totals), 'dp', scatter_dimension=0, tiled=True)  763 us
    unnamed x48, waiting for transfers between devices  300 us
    all_gather x1, waiting for transfers between devices, per_device(): lax.all_gather(w_gate[0], 'dp', axis=0, tiled=True)  174 us
    all_gather x1, waiting for transfers between devices, per_device(): lax.all_gather(w_up[0], 'dp', axis=0, tiled=True)  169 us
    all_gather x1, waiting for transfers between devices, per_device(): lax.all_gather(w_down[0], 'dp', axis=0, tiled=True)  168 us
    dot_general x21, matrix products, dot_first(): lax.dot_general(left, right, (((0,), (0,)), ((), ())), preferred_element_...  152 us
    dot_general x21, matrix products, dot_last(): lax.dot_general(left, right, (((1,), (1,)), ((), ())), preferred_element_...  110 us
    dot_general x21, matrix products, dot_plain(): return jnp.dot(left, right, preferred_element_type=jnp.float32)  99.3 us
  transfers between devices with their start and end apart: 46, of which 40 were waited for; matrix products, arithmetic and copies ran while one was open for 14% of the time, Pallas kernels for 0%

commit v1 on v0

--- a/solution.py
+++ b/solution.py
@@ -3,6 +3,8 @@
 import jax
 import jax.numpy as jnp
 from jax import lax
+from jax.experimental import pallas as pl
+from jax.experimental.pallas import tpu as pltpu
 from jax.sharding import PartitionSpec as P
 
 EPSILON = 1e-06
@@ -83,7 +85,7 @@
 
 
 def attend(queries, keys_all, values_all, allowed, head_size):
-    scores, query_heads, key_heads = scores_for(queries, keys_all, allowed, head_size)
+    scores, _, key_heads = scores_for(queries, keys_all, allowed, head_size)
     highest = jnp.max(scores, axis=-1, keepdims=True)
     weights = jnp.exp(scores - highest)
     total = jnp.sum(weights, axis=-1, keepdims=True)
@@ -121,7 +123,7 @@
     )
 
 
-def per_device(
+def per_device_wide(
     inputs,
     cotangent,
     segments,
@@ -359,9 +361,544 @@
     )
 
 
+def paired(x, axis, flip):
+    count = lax.axis_size(axis)
+    return lax.ppermute(x, axis, [(i, i ^ flip) for i in range(count)])
+
+
+def ring_order(count):
+    return list(range(0, count, 2)) + list(range(count - 1, 0, -2))
+
+
+def ring(x, by):
+    order = ring_order(lax.axis_size("dp"))
+    count = len(order)
+    pairs = []
+    for core, step in ((0, by), (1, -by)):
+        for i in range(count):
+            pairs.append((core * count + order[i], core * count + order[(i + step) % count]))
+    return lax.ppermute(x, ("tensor", "dp"), pairs)
+
+
+def received_order(count):
+    half = count // 2
+    return [(0, False)] + [(s, lag) for s in range(1, half) for lag in (False, True)] + [(half, False)]
+
+
+def near_chunks(count):
+    return 2 * (count // 2 - 2) + 1
+
+
+def gate(value, token):
+    return lax.optimization_barrier((value, token))[0]
+
+
+def whole_vmem(count):
+    return [pl.BlockSpec(memory_space=pltpu.VMEM)] * count
+
+
+def joined(pieces):
+    rows = sum(piece.shape[0] for piece in pieces)
+    width = pieces[0].shape[1]
+
+    def kernel(*refs):
+        at = 0
+        for ref in refs[:-1]:
+            refs[-1][at : at + ref.shape[0], :] = ref[...]
+            at += ref.shape[0]
+
+    return pl.pallas_call(
+        kernel,
+        out_shape=jax.ShapeDtypeStruct((rows, width), pieces[0].dtype),
+        in_specs=whole_vmem(len(pieces)),
+        out_specs=pl.BlockSpec(memory_space=pltpu.VMEM),
+        cost_estimate=pl.CostEstimate(flops=0, bytes_accessed=4 * rows * width, transcendentals=0),
+    )(*pieces)
+
+
+def gather_ring(chunk):
+    count = lax.axis_size("dp")
+    half = count // 2
+    lead, lag = chunk, paired(chunk, "tensor", 1)
+    chunks, token = [chunk], None
+    for step in range(1, half + 1):
+        lead = ring(lead, 1)
+        chunks.append(lead)
+        if step < half:
+            lag = ring(lag, 1)
+            chunks.append(lag)
+        if step == half - 1:
+            token = lead
+    cut = near_chunks(count)
+    near, far = joined(gate(chunks[:cut], token)), joined(chunks[cut:])
+    return [near, far, paired(near, "tensor", 1), paired(far, "tensor", 1)], token
+
+
+def multiplied(parts, weight):
+    return jnp.concatenate(parts, axis=0), by_parts(parts, weight)
+
+
+def by_parts(parts, weight):
+    return jnp.concatenate([dot_plain(part, weight) for part in parts], axis=0)
+
+
+def product_scattered(act, weight):
+    count = lax.axis_size("dp")
+    half = count // 2
+    side = act.shape[0] // 2
+    rows = side // count
+    near = near_chunks(count) * rows
+    far_sum = dot_last(act[side + near :], weight).astype(jnp.bfloat16)
+    near_sum = dot_last(act[side : side + near], weight).astype(jnp.bfloat16)
+    own = dot_last(act[:side], weight)
+    far_sum = paired(far_sum, "tensor", 1)
+    near_sum = paired(near_sum, "tensor", 1)
+    spots = {key: i * rows for i, key in enumerate(received_order(count))}
+
+    def part(hops, lag):
+        at = spots[hops, lag]
+        extra = far_sum[at - near :][:rows] if at >= near else near_sum[at : at + rows]
+        return own[at : at + rows] + extra.astype(jnp.float32)
+
+    def hop(value, hops, lag):
+        total = part(hops, lag)
+        if value is not None:
+            total = total + value.astype(jnp.float32)
+        return ring(total.astype(jnp.bfloat16), -1)
+
+    lead = lag = token = None
+    for hops in range(half, 0, -1):
+        lead = hop(lead, hops, False)
+        if hops < half:
+            lag = hop(lag, hops, True)
+        if hops == half - 1:
+            token = lead
+    across = paired(lag, "tensor", 1)
+    return part(0, False) + lead.astype(jnp.float32) + across.astype(jnp.float32), token
+
+
+def place_rows(blocks, flags, widths):
+    count = len(blocks)
+    rows, total = blocks[0].shape
+    part = rows // 2
+
+    def kernel(flags_ref, *refs):
+        for s in range(count):
+            left = 0
+            for out, width in zip(refs[count:], widths):
+                for half in range(2):
+                    at = pl.multiple_of((flags_ref[0] ^ s) * part + half * count * part, part)
+                    top = half * part
+                    out[pl.ds(at, part), :] = refs[s][top : top + part, left : left + width]
+                left += width
+
+    size = 2 * count * rows * total
+    return pl.pallas_call(
+        kernel,
+        out_shape=[jax.ShapeDtypeStruct((count * rows, w), blocks[0].dtype) for w in widths],
+        in_specs=[pl.BlockSpec(memory_space=pltpu.SMEM)] + whole_vmem(count),
+        out_specs=whole_vmem(len(widths)),
+        cost_estimate=pl.CostEstimate(flops=0, bytes_accessed=2 * size, transcendentals=0),
+    )(flags, *blocks)
+
+
+def place_columns(first, second, flags, widths, shared):
+    count = len(first)
+    rows = first[0].shape[0]
+    columns = [w * count // (2 if wide else 1) for w, wide in zip(widths, shared)]
+    total = sum(columns)
+
+    def kernel(flags_ref, *refs):
+        kept, sent = refs[2 * count :]
+
+        def fill(out, blocks):
+            left = base = 0
+            for width, wide, room in zip(widths, shared, columns):
+                for s in range(0, count, 2 if wide else 1):
+                    index = flags_ref[0] ^ s
+                    at = base + (index // 2 if wide else index) * width
+                    value = blocks[s][:, left : left + width]
+                    if wide:
+                        value = value.astype(jnp.float32) + blocks[s + 1][
+                            :, left : left + width
+                        ].astype(jnp.float32)
+                    out[:, pl.ds(pl.multiple_of(at, 128), width)] = value.astype(out.dtype)
+                left += width
+                base += room
+
+        @pl.when(flags_ref[1] == 0)
+        def _():
+            fill(kept, refs[:count])
+            fill(sent, refs[count : 2 * count])
+
+        @pl.when(flags_ref[1] != 0)
+        def _():
+            fill(sent, refs[:count])
+            fill(kept, refs[count : 2 * count])
+
+    return pl.pallas_call(
+        kernel,
+        out_shape=[jax.ShapeDtypeStruct((rows, total), first[0].dtype)] * 2,
+        in_specs=[pl.BlockSpec(memory_space=pltpu.SMEM)] + whole_vmem(2 * count),
+        out_specs=whole_vmem(2),
+        cost_estimate=pl.CostEstimate(
+            flops=0, bytes_accessed=4 * count * rows * sum(widths) * 2, transcendentals=0
+        ),
+    )(flags, *first, *second)
+
+
+def head_attend(query, key, value, allowed):
+    scores = dot_last(query, key) * query.shape[1] ** (-0.5)
+    scores = jnp.where(allowed, scores, MASKED)
+    highest = jnp.max(scores, axis=-1, keepdims=True)
+    weights = jnp.exp(scores - highest)
+    total = jnp.sum(weights, axis=-1, keepdims=True)
+    probs = (weights / total).astype(jnp.bfloat16)
+    return dot_plain(probs, value).astype(jnp.bfloat16), highest + jnp.log(total)
+
+
+def head_attend_back(query, key, value, allowed, log_total, grad):
+    scale = query.shape[1] ** (-0.5)
+    scores = jnp.where(allowed, dot_last(query, key) * scale, MASKED)
+    probs = jnp.exp(scores - log_total)
+    prob_grad = dot_last(grad, value)
+    delta = jnp.sum(probs * prob_grad, axis=-1, keepdims=True)
+    score_grad = (probs * (prob_grad - delta)).astype(jnp.bfloat16)
+    return (
+        dot_plain(score_grad, key) * scale,
+        dot_first(score_grad, query) * scale,
+        dot_first(probs.astype(jnp.bfloat16), grad),
+    )
+
+
+def per_device(
+    inputs,
+    cotangent,
+    segments,
+    w_query,
+    key_weight,
+    value_weight,
+    w_output,
+    w_gate,
+    w_up,
+    w_down,
+    attn_gain,
+    mlp_gain,
+    query_gain,
+    key_gain,
+):
+    count = lax.axis_size("dp")
+    plane = lax.axis_index("section")
+    me = lax.axis_index("dp")
+    core = lax.axis_index("tensor")
+    flags = jnp.stack([me, plane]).astype(jnp.int32)
+    model_width = inputs.shape[2]
+    rows = inputs.shape[1] // 2
+    head_size = query_gain.shape[1]
+    ff_width = w_gate.shape[2] // count
+    group_size = w_query.shape[2] // key_weight.shape[2]
+    gain_width = attn_gain.shape[1]
+
+    def by_layer(own):
+        theirs = paired(own, "section", 1)
+        first = plane == 0
+        return [jnp.where(first, own, theirs), jnp.where(first, theirs, own)]
+
+    part = gain_width // 2
+
+    def halved(array):
+        wide = array.reshape(-1, count, 2, part)
+        return jnp.swapaxes(wide, 1, 2).reshape(array.shape)
+
+    def unhalved(array):
+        wide = array.reshape(-1, 2, count, part)
+        return jnp.swapaxes(wide, 1, 2).reshape(array.shape)
+
+    def own_rows(array):
+        own = lax.dynamic_slice(array, (plane, core * rows, 0), (1, rows, model_width))[0]
+        return halved(own)
+
+    gains = jnp.concatenate([attn_gain[0], mlp_gain[0], query_gain[0], key_gain[0]])
+    gains = jnp.concatenate(by_layer(gains.astype(jnp.float32)))
+    docs = lax.dynamic_index_in_dim(segments, plane, 0, keepdims=False).astype(jnp.float32)
+    note = jnp.concatenate([gains, docs])
+    notes = jnp.stack([note] + [paired(note, "dp", s) for s in range(1, count)])
+    notes = jnp.concatenate(
+        [lax.dynamic_slice_in_dim(notes, me ^ j, 1, axis=0) for j in range(count)], axis=0
+    )
+    per_layer = gains.shape[0] // 2
+    layer_gains = []
+    for layer in range(2):
+        at = layer * per_layer
+        layer_gains.append(
+            (
+                halved(notes[:, at : at + gain_width].reshape(-1)),
+                halved(notes[:, at + gain_width : at + 2 * gain_width].reshape(-1)),
+                gains[at + 2 * gain_width : at + 2 * gain_width + head_size],
+                gains[at + 2 * gain_width + head_size : at + per_layer],
+            )
+        )
+    doc_table = notes[:, 2 * per_layer :].reshape(count, 2, rows)
+
+    place = jnp.where(me % 2 == 0, me // 2, count - 1 - me // 2)
+    docs_parts, pos_parts = ([], []), ([], [])
+    away = 2 * core - 1
+    for at in range(2):
+        for hops, lag in received_order(count):
+            side = core if lag == bool(at) else 1 - core
+            spot = (place + (away if at == 0 else -away) * hops + count) % count
+            owner = jnp.where(spot < count // 2, 2 * spot, 2 * (count - 1 - spot) + 1)
+            block = lax.dynamic_index_in_dim(doc_table, owner, 0, keepdims=False)
+            docs_parts[at].append(lax.dynamic_index_in_dim(block, side, 0, keepdims=False))
+            start = owner * 2 * rows + side * rows
+            pos_parts[at].append(start + jnp.arange(rows, dtype=jnp.int32))
+    docs_all = jnp.concatenate(docs_parts[0] + docs_parts[1])
+    positions = jnp.concatenate(pos_parts[0] + pos_parts[1])
+    allowed = (positions[None, :] <= positions[:, None]) & (docs_all[:, None] == docs_all[None, :])
+    cosine, sine_table = rope_tables(positions, head_size)
+    rope = partial(rotate_norm, cosine=cosine, sine_table=sine_table)
+
+    def cut(pieces):
+        def block(to):
+            return jnp.concatenate(
+                [
+                    lax.dynamic_slice_in_dim(array, (to // share) * width, width, axis=1)
+                    for array, width, share in pieces
+                ],
+                axis=1,
+            )
+
+        return [block(me ^ s) for s in range(count)]
+
+    def turn(blocks):
+        return [blocks[0]] + [paired(blocks[s], "dp", s) for s in range(1, count)]
+
+    def both_layers(blocks, widths):
+        sets = []
+        for placed in place_rows(blocks, flags, widths):
+            facing = paired(placed, "section", 1)
+            sets.append([jnp.where(plane == layer, placed, facing) for layer in range(2)])
+        return sets
+
+    pieces_of = {
+        "qk": ((w_query[0], head_size, 1), (key_weight[0], head_size, group_size)),
+        "vo": ((value_weight[0], head_size, group_size), (w_output[0], head_size, 1)),
+        "g": ((w_gate[0], ff_width, 1),),
+        "u": ((w_up[0], ff_width, 1),),
+        "d": ((w_down[0], ff_width, 1),),
+    }
+    sliced = {name: cut(pieces) for name, pieces in pieces_of.items()}
+    turned, weights = {}, {}
+
+    def attention(raw, value, layer):
+        _, _, gain_q, gain_k = layer_gains[layer]
+        queries, key_raw = raw[:, :head_size], raw[:, head_size:]
+        value = value.astype(jnp.bfloat16)
+        query_rot = rope(queries, gain_q).astype(jnp.bfloat16)
+        key_rot = rope(key_raw, gain_k).astype(jnp.bfloat16)
+        attn, log_total = head_attend(query_rot, key_rot, value, allowed)
+        return attn, (queries, key_raw, value, query_rot, key_rot, log_total)
+
+    def forward(layer_in, layer):
+        gain_attn, gain_mlp, _, _ = layer_gains[layer]
+        if layer == 0:
+            turned["qk"] = turn(sliced["qk"])
+            parts, token = gather_ring(layer_in.astype(jnp.bfloat16))
+            raw_in = joined(parts).astype(jnp.float32)
+            weights["qk"] = both_layers(turned["qk"], (2 * head_size,))[0]
+            turned["vo"] = turn(gate(sliced["vo"], turned["qk"]))
+            weights["v"], weights["o"] = both_layers(turned["vo"], (head_size, head_size))
+            turned["g"] = turn(gate(sliced["g"], turned["vo"]))
+            normed = rms_scale(raw_in, gain_attn).astype(jnp.bfloat16)
+            raw = dot_plain(normed, weights["qk"][0])
+            value = dot_plain(normed, weights["v"][0])
+        else:
+            chunk = rms_scale(layer_in, gain_attn).astype(jnp.bfloat16)
+            parts, token = gather_ring(chunk)
+            normed, raw = multiplied(parts, weights["qk"][layer])
+            value = by_parts(parts, weights["v"][layer])
+        attn, kept = attention(raw, value, layer)
+        if layer == 0:
+            weights["g"] = both_layers(gate(turned["g"], attn), (ff_width,))[0]
+            turned["u"] = turn(gate(sliced["u"], turned["g"]))
+            extra = None
+        else:
+            cotangent_rows = own_rows(cotangent)
+            extra, token = gather_ring(gate(cotangent_rows, raw))
+            attn = gate(attn, token)
+        summed, token = product_scattered(attn, weights["o"][layer])
+        mixed = layer_in + summed
+        if layer == 0:
+            weights["u"] = both_layers(gate(turned["u"], mixed), (ff_width,))[0]
+            turned["d"] = turn(gate(sliced["d"], turned["u"]))
+            weights["gu"] = [
+                jnp.concatenate([weights["g"][i], weights["u"][i]], axis=1) for i in range(2)
+            ]
+        parts, token = gather_ring(rms_scale(mixed, gain_mlp).astype(jnp.bfloat16))
+        if layer == 0:
+            weights["d"] = both_layers(gate(turned["d"], parts[1]), (ff_width,))[0]
+        normed_mlp, raw_mlp = multiplied(parts, weights["gu"][layer])
+        gate_raw, up_raw = raw_mlp[:, :ff_width], raw_mlp[:, ff_width:]
+        activated = swiglu(gate_raw, up_raw).astype(jnp.bfloat16)
+        summed, token = product_scattered(activated, weights["d"][layer])
+        stored = (layer_in, normed, kept, attn, mixed, normed_mlp, gate_raw, up_raw, activated)
+        return mixed + summed, stored, extra
+
+    def halves(grad):
+        span = grad.shape[0] // 2
+        sent = lax.dynamic_slice_in_dim(grad, (1 - plane) * span, span, axis=0)
+        kept = lax.dynamic_slice_in_dim(grad, plane * span, span, axis=0)
+        return kept, paired(sent.astype(jnp.bfloat16), "section", 1)
+
+    last_turn = []
+
+    def returned(pair, token):
+        kept, taken = pair
+        if token is not None:
+            taken = gate(taken, token)
+        total = (kept + taken.astype(jnp.float32)).astype(jnp.bfloat16)
+        blocks = [lax.dynamic_slice_in_dim(total, (me ^ s) * part, part, axis=0) for s in range(count)]
+        if last_turn:
+            blocks = gate(blocks, last_turn[-1])
+        last_turn.append(turn(blocks))
+        return last_turn[-1]
+
+    def backward(gathered, grad_out, stored, layer, back):
+        layer_in, normed, kept, attn, mixed, normed_mlp, gate_raw, up_raw, activated = stored
+        queries, key_raw, value, query_rot, key_rot, log_total = kept
+        gain_attn, gain_mlp, gain_q, gain_k = layer_gains[layer]
+        out_low, act_grad = multiplied(gathered, weights["d"][layer])
+        unused, swiglu_back = jax.vjp(swiglu, gate_raw, up_raw)
+        gate_grad, up_grad = swiglu_back(act_grad)
+        raw_grad = jnp.concatenate([gate_grad, up_grad], axis=1).astype(jnp.bfloat16)
+        summed, token = product_scattered(raw_grad, weights["gu"][layer])
+        sums = {}
+        sums["d"] = halves(dot_first(out_low, activated))
+        sums["gu"] = halves(dot_first(normed_mlp, raw_grad))
+        back["d"] = returned(sums["d"], token)
+        unused, mlp_norm_back = jax.vjp(rms_scale, mixed, gain_mlp)
+        mixed_part, grad_gain_mlp = mlp_norm_back(summed)
+        mixed_grad = grad_out + mixed_part
+        parts, token = gather_ring(mixed_grad.astype(jnp.bfloat16))
+        branch_low, attn_grad = multiplied(parts, weights["o"][layer])
+        back["gu"] = returned(sums["gu"], parts[0])
+        query_back, key_back, value_back = head_attend_back(
+            query_rot, key_rot, value, allowed, log_total, attn_grad.astype(jnp.bfloat16)
+        )
+        unused, key_rope_back = jax.vjp(rope, key_raw, gain_k)
+        key_grad, grad_gain_k = key_rope_back(key_back)
+        unused, query_rope_back = jax.vjp(rope, queries, gain_q)
+        query_grad, grad_gain_q = query_rope_back(query_back)
+        qkv_grad = jnp.concatenate([query_grad, key_grad, value_back], axis=1).astype(jnp.bfloat16)
+        summed, token = product_scattered(qkv_grad, weights["qkv"][layer])
+        grad_attn = [dot_first(normed, qkv_grad), dot_first(branch_low, attn)]
+        sums["attn"] = halves(jnp.concatenate(grad_attn, axis=1))
+        unused, attn_norm_back = jax.vjp(rms_scale, layer_in, gain_attn)
+        input_part, grad_gain_attn = attn_norm_back(summed)
+        small = (grad_gain_attn, grad_gain_mlp, grad_gain_q, grad_gain_k)
+        points = (mixed_grad, branch_low, qkv_grad)
+        return mixed_grad + input_part, sums["attn"], small, points
+
+    out_first, stored_first, _ = forward(own_rows(inputs).astype(jnp.float32), 0)
+    out_first = out_first.astype(jnp.bfloat16)
+    weights["qkv"] = [
+        jnp.concatenate([weights["qk"][i], weights["v"][i]], axis=1) for i in range(2)
+    ]
+    out_second, stored_second, gathered = forward(out_first.astype(jnp.float32), 1)
+    out_second = out_second.astype(jnp.bfloat16)
+    back_second, back_first = {}, {}
+    grad_second, late, small_second, points = backward(
+        gathered, own_rows(cotangent).astype(jnp.float32), stored_second, 1, back_second
+    )
+    grad_second = grad_second.astype(jnp.bfloat16)
+    gathered, token = gather_ring(grad_second)
+    back_second["attn"] = returned(late, token)
+    grad_first, late, small_first, points = backward(
+        gathered, grad_second.astype(jnp.float32), stored_first, 0, back_first
+    )
+    grad_first = grad_first.astype(jnp.bfloat16)
+    back_first["attn"] = returned(late, None)
+
+    def by_section(first, second):
+        first, second = unhalved(first), unhalved(second)
+        kept = jnp.where(plane == 0, first, second)
+        taken = paired(jnp.where(plane == 0, second, first), "section", 1)
+        both = jnp.where(plane == 0, jnp.stack([kept, taken]), jnp.stack([taken, kept]))
+        facing = paired(both, "tensor", 1)
+        return jnp.where(
+            core == 0,
+            jnp.concatenate([both, facing], axis=1),
+            jnp.concatenate([facing, both], axis=1),
+        )[None]
+
+    section_out = by_section(out_first, out_second)
+    input_grads = by_section(grad_first, grad_second)
+
+    def owned(name, widths, shared, token):
+        firsts = back_first[name] if token is None else gate(back_first[name], token)
+        kept, sent = place_columns(firsts, back_second[name], flags, widths, shared)
+        taken = paired(sent, "section", 1)
+        both = jnp.where(
+            plane == 0,
+            jnp.concatenate([kept, taken], axis=0),
+            jnp.concatenate([taken, kept], axis=0),
+        )
+        return both.astype(jnp.float32)
+
+    _, branch_point, summed_point = points
+    ff_total = w_gate.shape[2]
+    grad_d = owned("d", (ff_width,), (False,), branch_point)
+    grad_gu = owned("gu", (ff_width,) * 2, (False,) * 2, summed_point)
+    grad_attn = owned("attn", (head_size,) * 4, (False, True, True, False), None)
+    edges = [0]
+    for array in (w_query, key_weight, value_weight, w_output):
+        edges.append(edges[-1] + array.shape[2])
+    attn_grads = [grad_attn[:, a:b] for a, b in zip(edges, edges[1:])]
+    mlp_grads = (grad_gu[:, :ff_total], grad_gu[:, ff_total:], grad_d)
+
+    rows_of = jnp.concatenate(
+        [
+            part.reshape(count, -1)
+            for small in (small_first, small_second)
+            for part in (
+                unhalved(small[0]),
+                unhalved(small[1]),
+                jnp.tile(small[2], count),
+                jnp.tile(small[3], count),
+            )
+        ],
+        axis=1,
+    )
+
+    def row(to):
+        return lax.dynamic_index_in_dim(rows_of, to, 0, keepdims=False)
+
+    gain_sum = row(me)
+    for s in range(1, count):
+        gain_sum = gain_sum + paired(row(me ^ s), "dp", s)
+    gain_sum = gain_sum + paired(gain_sum, "tensor", 1)
+    gain_sum = gain_sum + paired(gain_sum, "section", 1)
+    mine = jnp.where(plane == 0, gain_sum[:per_layer], gain_sum[per_layer:])
+    grad_gain_attn = mine[:gain_width]
+    grad_gain_mlp = mine[gain_width : 2 * gain_width]
+    grad_gain_q = mine[2 * gain_width : 2 * gain_width + head_size]
+    grad_gain_k = mine[2 * gain_width + head_size :]
+    shards = (
+        attn_grads[0], attn_grads[1], attn_grads[2], attn_grads[3],
+        mlp_grads[0], mlp_grads[1], mlp_grads[2],
+        grad_gain_attn, grad_gain_mlp, grad_gain_q, grad_gain_k,
+    )
+    return (section_out, input_grads) + tuple(part[None] for part in shards)
+
+
+def fits(mesh):
+    sizes = dict(mesh.shape)
+    return sizes["dp"] == 8 and sizes["tensor"] == 2 and sizes["section"] == 2
+
+
 def solution(mesh):
     return jax.shard_map(
-        per_device,
+        per_device if fits(mesh) else per_device_wide,
         mesh=mesh,
         in_specs=(
             P(None, "dp", None),

time: 3060 us -> 1130 us (0.37)
  waiting for transfers between devices: 2250 us -> 439 us
  starting transfers between devices: 25.2 us -> 324 us
  matrix products: 412 us -> 118 us
  blocking collectives: 110 us -> 0 us
  Pallas kernels: 0 us -> 68.4 us
  local copies, waits for them, and re-layouts: 98.5 us -> 54.6 us
    all_gather x17 -> x0, waiting for transfers between devices: 988 us -> none  [the longest x1 174 us: per_device(): lax.all_gather(w_gate[0], 'dp', axis=0, tiled=True)]
    reduce_scatter x7 -> x0, waiting for transfers between devices: 763 us -> none  [per_device(): lax.psum_scatter(as_sent(totals), 'dp', scatter_dimension=0, tiled=True)]
    ppermute x4 -> x273, waiting for transfers between devices: 37.4 us -> 439 us  [the longest x112 235 us: ring(): return lax.ppermute(x, ('tensor', 'dp'), pairs)]
    ppermute x4 -> x273, starting transfers between devices: 10.5 us -> 324 us  [the longest x161 194 us: paired(): return lax.ppermute(x, axis, [(i, i ^ flip) for i in range(count)])]
    unnamed x48 -> x0, waiting for transfers between devices: 300 us -> none
    psum x12 -> x0, waiting for transfers between devices: 162 us -> none  [the longest x3 51.8 us: per_device(): lax.psum((dot_last(gate_grad, w_g) + dot_last(up_grad, w_u)).astype(jnp.b...]
    dot_general x21 -> x12, matrix products: 152 us -> 31.5 us  [dot_first(): lax.dot_general(left, right, (((0,), (0,)), ((), ())), preferred_element_...]
    dot_general x21 -> x28, matrix products: 110 us -> 33.4 us  [dot_last(): lax.dot_general(left, right, (((1,), (1,)), ((), ())), preferred_element_...]
  transfers between devices with their start and end apart: 46 -> 273, of which waited for: 40 -> 119; matrix products, arithmetic and copies ran while one was open for 14% -> 19% of each run, Pallas kernels for 0% -> 5%
where the time goes in v1:
time: 1130 us; the launch traced here: 1120 us
  waiting for transfers between devices  439 us (39%)
  starting transfers between devices  324 us (29%)
  matrix products  118 us (10%)
  other arithmetic  113 us (10%)
  Pallas kernels  68.4 us (6%)
  local copies, waits for them, and re-layouts  54.6 us (5%)
    ppermute x112, waiting for transfers between devices, ring(): return lax.ppermute(x, ('tensor', 'dp'), pairs)  235 us
    ppermute x161, waiting for transfers between devices, paired(): return lax.ppermute(x, axis, [(i, i ^ flip) for i in range(count)])  204 us
    ppermute x161, starting transfers between devices, paired(): return lax.ppermute(x, axis, [(i, i ^ flip) for i in range(count)])  194 us
    ppermute x112, starting transfers between devices, ring(): return lax.ppermute(x, ('tensor', 'dp'), pairs)  129 us
    dot_general x37, matrix products, dot_plain(): return jnp.dot(left, right, preferred_element_type=jnp.float32)  53.2 us
    pallas_call x17, Pallas kernels, joined(): pl.pallas_call(kernel, out_shape=jax.ShapeDtypeStruct((rows, width), piec...  41 us
    dot_general x28, matrix products, dot_last(): lax.dot_general(left, right, (((1,), (1,)), ((), ())), preferred_element_...  33.4 us
    dot_general x12, matrix products, dot_first(): lax.dot_general(left, right, (((0,), (0,)), ((), ())), preferred_element_...  31.5 us
  transfers between devices with their start and end apart: 273, of which 119 were waited for; matrix products, arithmetic and copies ran while one was open for 19% of the time, Pallas kernels for 5%

profile of v1, /device:TPU:0, one launch (start us, length us, event | category | flops | bytes accessed | tf_op | source)
XLA Modules:
  0.0 1123.1 jit_solution(4091354283254279497)
XLA Ops:
  60.5 6.7 collective-permute-start.30
  107.4 17.1 %collective-permute-done.34 = bf16[2048,128]{1,0:T(8,128)(2,1)} collective-permute-done((bf16[2048,128]{1,0:T(8,128)(2,1)S(1)}, bf16[2048,128]{1,0:T(8,128)(2,1)}, u32[]{:S(2)}, u32[]{:S(2)}) %collective-permute-start.34) | collective-permute-done | bytes 524320 | tf_op jit(solution)/shard_map/ppermute | solution.py:366
  157.6 7.4 collective-permute-done.37
  179.3 6.3 collective-permute-done.42
  210.9 12.9 %collective-permute-done.55.refs_5_ = bf16[256,384]{1,0:T(8,128)(2,1)S(1)} collective-permute-done((bf16[256,384]{1,0:T(8,128)(2,1)S(1)}, bf16[256,384]{1,0:T(8,128)(2,1)S(1)}, u32[]{:S(2)}, u32[]{:S(2)}) %collective-permute-start.55) | collective-permute-done | bytes 196640 | tf_op jit(solution)/shard_map/ppermute | solution.py:366
  226.3 7.0 collective-permute-start.60
  249.3 12.0 %collective-permute-done.62.refs_4_ = bf16[256,384]{1,0:T(8,128)(2,1)} collective-permute-done((bf16[256,384]{1,0:T(8,128)(2,1)}, bf16[256,384]{1,0:T(8,128)(2,1)}, u32[]{:S(2)}, u32[]{:S(2)}) %collective-permute-start.62) | collective-permute-done | bytes 196640 | tf_op jit(solution)/shard_map/ppermute | solution.py:366
  269.6 7.8 collective-permute-start.47
  296.5 12.7 %collective-permute-done.73.refs_3_ = bf16[256,384]{1,0:T(8,128)(2,1)S(1)} collective-permute-done((bf16[256,384]{1,0:T(8,128)(2,1)S(1)}, bf16[256,384]{1,0:T(8,128)(2,1)S(1)}, u32[]{:S(2)}, u32[]{:S(2)}) %collective-permute-start.73) | collective-permute-done | bytes 196640 | tf_op jit(solution)/shard_map/ppermute | solution.py:366
  348.0 24.5 %collective-permute-done.78 = bf16[2048,384]{1,0:T(8,128)(2,1)S(1)} collective-permute-done((bf16[2048,384]{1,0:T(8,128)(2,1)}, bf16[2048,384]{1,0:T(8,128)(2,1)S(1)}, u32[]{:S(2)}, u32[]{:S(2)}) %collective-permute-start.78) | collective-permute-done | bytes 1572896 | tf_op jit(solution)/shard_map/ppermute | solution.py:366
  378.8 8.3 collective-permute-done.81
  387.5 6.3 collective-permute-done.82
  400.8 6.4 collective-permute-done.86
  407.4 6.3 collective-permute-done.87
  583.9 6.2 collective-permute-done.143
  603.7 6.2 collective-permute-done.148
  784.8 6.2 collective-permute-start.223
  813.0 7.5 collective-permute-done.130
  892.8 8.3 collective-permute-done.236.refs_12_
  942.9 6.9 collective-permute-done.244.refs_5_
  975.5 6.7 pad_maximum_fusion
  998.3 12.1 %collective-permute-done.251.refs_5_ = bf16[128,768]{1,0:T(8,128)(2,1)S(1)} collective-permute-done((bf16[128,768]{1,0:T(8,128)(2,1)S(1)}, bf16[128,768]{1,0:T(8,128)(2,1)S(1)}, u32[]{:S(2)}, u32[]{:S(2)}) %collective-permute-start.251) | collective-permute-done | bytes 196640 | tf_op jit(solution)/shard_map/ppermute | solution.py:366
  1028.5 7.3 collective-permute-start.254
  1054.5 7.5 collective-permute-done.257.refs_4_
  (1529 shorter events, 900.6 us)
Async XLA Ops:
  8.2 32.1 %collective-permute-start.24 = (bf16[256,256]{1,0:T(8,128)(2,1)S(1)}, bf16[256,256]{1,0:T(8,128)(2,1)S(1)}, u32[]{:S(2)}, u32[]{:S(2)}) collective-permute-start(bf16[256,256]{1,0:T(8,128)(2,1)S(1)} %pad_maximum_fusion.33), channel_id=1, source_target_pairs={{0,7},{1,6},{2,5},{3,4},{4,3},{5,2},{6,1},{7,0},{8,15},{9,14},{10,... | collective-permute-start | bytes 393224 | tf_op jit(solution)/shard_map/ppermute | solution.py:366
  90.6 35.9 %collective-permute-start.25 = (bf16[2048,256]{1,0:T(8,128)(2,1)}, bf16[2048,256]{1,0:T(8,128)(2,1)}, u32[]{:S(2)}, u32[]{:S(2)}) collective-permute-start(bf16[2048,256]{1,0:T(8,128)(2,1)} %shard_map.240), channel_id=1, source_target_pairs={{0,16},{16,0},{1,17},{17,1},{2,18},{18,2},{3,19},{19,3},{4,20},{20... | collective-permute-start | bytes 3145736 | tf_op jit(solution)/shard_map/ppermute | solution.py:366
  92.1 32.4 %collective-permute-start.34 = (bf16[2048,128]{1,0:T(8,128)(2,1)S(1)}, bf16[2048,128]{1,0:T(8,128)(2,1)}, u32[]{:S(2)}, u32[]{:S(2)}) collective-permute-start(bf16[2048,128]{1,0:T(8,128)(2,1)S(1)} %copy-done.140), channel_id=1, source_target_pairs={{0,16},{16,0},{1,17},{17,1},{2,18},{18,2},{3,19},{19,3},{4,20},{20... | collective-permute-start | bytes 1572872 | tf_op jit(solution)/shard_map/ppermute | solution.py:366
  95.2 35.0 %collective-permute-start.16 = (bf16[320,2048]{1,0:T(8,128)(2,1)}, bf16[320,2048]{1,0:T(8,128)(2,1)}, u32[]{:S(2)}, u32[]{:S(2)}) collective-permute-start(bf16[320,2048]{1,0:T(8,128)(2,1)} %shard_map.237.refs_0_), channel_id=1, source_target_pairs={{0,8},{8,0},{1,9},{9,1},{2,10},{10,2},{3,11},{11,3},{4,12},{12,4},... | collective-permute-start | bytes 3932168 | tf_op jit(solution)/shard_map/ppermute | solution.py:366
  194.8 41.3 %collective-permute-start.40 = (bf16[64,2048]{1,0:T(8,128)(2,1)S(1)}, bf16[64,2048]{1,0:T(8,128)(2,1)S(1)}, u32[]{:S(2)}, u32[]{:S(2)}) collective-permute-start(bf16[64,2048]{1,0:T(8,128)(2,1)S(1)} %get-tuple-element.413), channel_id=1, source_target_pairs={{0,1},{2,0},{4,2},{6,4},{7,6},{5,7},{3,5},{1,3},{8,10},{10,12},{12... | collective-permute-start | bytes 786440 | tf_op jit(solution)/shard_map/ppermute | solution.py:380
  198.0 41.9 %collective-permute-start.44 = (bf16[64,2048]{1,0:T(8,128)(2,1)}, bf16[64,2048]{1,0:T(8,128)(2,1)S(1)}, u32[]{:S(2)}, u32[]{:S(2)}) collective-permute-start(bf16[64,2048]{1,0:T(8,128)(2,1)} %collective-permute-done.43), channel_id=1, source_target_pairs={{0,8},{8,0},{1,9},{9,1},{2,10},{10,2},{3,11},{11,3},{4,12},{12,4},... | collective-permute-start | bytes 786440 | tf_op jit(solution)/shard_map/ppermute | solution.py:366
  239.9 69.3 %collective-permute-start.58 = (bf16[2048,384]{1,0:T(8,128)(2,1)}, bf16[2048,384]{1,0:T(8,128)(2,1)S(1)}, u32[]{:S(2)}, u32[]{:S(2)}) collective-permute-start(bf16[2048,384]{1,0:T(8,128)(2,1)} %shard_map.243), channel_id=1, source_target_pairs={{0,16},{16,0},{1,17},{17,1},{2,18},{18,2},{3,19},{19,3},{4,20},{20... | collective-permute-start | bytes 4718600 | tf_op jit(solution)/shard_map/ppermute | solution.py:366
  269.4 67.4 %collective-permute-start.66 = (bf16[2048,384]{1,0:T(8,128)(2,1)}, bf16[2048,384]{1,0:T(8,128)(2,1)}, u32[]{:S(2)}, u32[]{:S(2)}) collective-permute-start(bf16[2048,384]{1,0:T(8,128)(2,1)} %shard_map.244), channel_id=1, source_target_pairs={{0,16},{16,0},{1,17},{17,1},{2,18},{18,2},{3,19},{19,3},{4,20},{20... | collective-permute-start | bytes 4718600 | tf_op jit(solution)/shard_map/ppermute | solution.py:366
  335.5 37.0 %collective-permute-start.78 = (bf16[2048,384]{1,0:T(8,128)(2,1)}, bf16[2048,384]{1,0:T(8,128)(2,1)S(1)}, u32[]{:S(2)}, u32[]{:S(2)}) collective-permute-start(bf16[2048,384]{1,0:T(8,128)(2,1)} %shard_map.246), channel_id=1, source_target_pairs={{0,16},{16,0},{1,17},{17,1},{2,18},{18,2},{3,19},{19,3},{4,20},{20... | collective-permute-start | bytes 4718600 | tf_op jit(solution)/shard_map/ppermute | solution.py:366
  524.9 41.4 %collective-permute-start.139 = (bf16[320,2048]{1,0:T(8,128)(2,1)}, bf16[320,2048]{1,0:T(8,128)(2,1)}, u32[]{:S(2)}, u32[]{:S(2)}) collective-permute-start(bf16[320,2048]{1,0:T(8,128)(2,1)} %shard_map.251), channel_id=1, source_target_pairs={{0,8},{8,0},{1,9},{9,1},{2,10},{10,2},{3,11},{11,3},{4,12},{12,4},... | collective-permute-start | bytes 3932168 | tf_op jit(solution)/shard_map/ppermute | solution.py:366
  688.3 35.8 %collective-permute-start.218 = (bf16[1024,384]{1,0:T(8,128)(2,1)S(1)}, bf16[1024,384]{1,0:T(8,128)(2,1)S(1)}, u32[]{:S(2)}, u32[]{:S(2)}) collective-permute-start(bf16[1024,384]{1,0:T(8,128)(2,1)S(1)} %dynamic-slice_convert_fusion.2), channel_id=1, source_target_pairs={{0,16},{16,0},{1,17},{17,1},{2,18},{18,2},{3,19},{19,3},{4,20},{20... | collective-permute-start | bytes 2359304 | tf_op jit(solution)/shard_map/ppermute | solution.py:366
  724.1 56.8 %collective-permute-start.217 = (bf16[1024,768]{1,0:T(8,128)(2,1)}, bf16[1024,768]{1,0:T(8,128)(2,1)}, u32[]{:S(2)}, u32[]{:S(2)}) collective-permute-start(bf16[1024,768]{1,0:T(8,128)(2,1)} %dynamic-slice_convert_fusion), channel_id=1, source_target_pairs={{0,16},{16,0},{1,17},{17,1},{2,18},{18,2},{3,19},{19,3},{4,20},{20... | collective-permute-start | bytes 4718600 | tf_op jit(solution)/shard_map/ppermute | solution.py:366
  740.6 50.5 %collective-permute-start.225 = (bf16[128,384]{1,0:T(8,128)(2,1)}, bf16[128,384]{1,0:T(8,128)(2,1)S(1)}, u32[]{:S(2)}, u32[]{:S(2)}) collective-permute-start(bf16[128,384]{1,0:T(8,128)(2,1)} %get-tuple-element.520), channel_id=1, source_target_pairs={{0,7},{1,6},{2,5},{3,4},{4,3},{5,2},{6,1},{7,0},{8,15},{9,14},{10,... | collective-permute-start | bytes 294920 | tf_op jit(solution)/shard_map/ppermute | solution.py:366
  774.2 34.8 %collective-permute-start.216 = (bf16[1024,512]{1,0:T(8,128)(2,1)S(1)}, bf16[1024,512]{1,0:T(8,128)(2,1)S(1)}, u32[]{:S(2)}, u32[]{:S(2)}) collective-permute-start(bf16[1024,512]{1,0:T(8,128)(2,1)S(1)} %fusion.60), channel_id=1, source_target_pairs={{0,16},{16,0},{1,17},{17,1},{2,18},{18,2},{3,19},{19,3},{4,20},{20... | collective-permute-start | bytes 3145736 | tf_op jit(solution)/shard_map/ppermute | solution.py:366
  778.0 34.4 %collective-permute-start.181 = (bf16[320,2048]{1,0:T(8,128)(2,1)S(1)}, bf16[320,2048]{1,0:T(8,128)(2,1)S(1)}, u32[]{:S(2)}, u32[]{:S(2)}) collective-permute-start(bf16[320,2048]{1,0:T(8,128)(2,1)S(1)} %convolution_convert_fusion.3), channel_id=1, source_target_pairs={{0,8},{8,0},{1,9},{9,1},{2,10},{10,2},{3,11},{11,3},{4,12},{12,4},... | collective-permute-start | bytes 3932168 | tf_op jit(solution)/shard_map/ppermute | solution.py:366
  870.1 57.0 %collective-permute-start.214 = (bf16[1024,768]{1,0:T(8,128)(2,1)}, bf16[1024,768]{1,0:T(8,128)(2,1)}, u32[]{:S(2)}, u32[]{:S(2)}) collective-permute-start(bf16[1024,768]{1,0:T(8,128)(2,1)} %dynamic-slice_convert_fusion.1), channel_id=1, source_target_pairs={{0,16},{16,0},{1,17},{17,1},{2,18},{18,2},{3,19},{19,3},{4,20},{20... | collective-permute-start | bytes 4718600 | tf_op jit(solution)/shard_map/ppermute | solution.py:366
  926.2 33.0 %collective-permute-start.199 = (bf16[320,2048]{1,0:T(8,128)(2,1)}, bf16[320,2048]{1,0:T(8,128)(2,1)}, u32[]{:S(2)}, u32[]{:S(2)}) collective-permute-start(bf16[320,2048]{1,0:T(8,128)(2,1)} %shard_map.257), channel_id=1, source_target_pairs={{0,8},{8,0},{1,9},{9,1},{2,10},{10,2},{3,11},{11,3},{4,12},{12,4},... | collective-permute-start | bytes 3932168 | tf_op jit(solution)/shard_map/ppermute | solution.py:366
  949.8 38.9 %collective-permute-start.247 = (bf16[128,768]{1,0:T(8,128)(2,1)S(1)}, bf16[128,768]{1,0:T(8,128)(2,1)S(1)}, u32[]{:S(2)}, u32[]{:S(2)}) collective-permute-start(bf16[128,768]{1,0:T(8,128)(2,1)S(1)} %get-tuple-element.310), channel_id=1, source_target_pairs={{0,1},{1,0},{2,3},{3,2},{4,5},{5,4},{6,7},{7,6},{8,9},{9,8},{10,11... | collective-permute-start | bytes 589832 | tf_op jit(solution)/shard_map/ppermute | solution.py:366
  951.9 38.9 %collective-permute-start.248 = (bf16[128,768]{1,0:T(8,128)(2,1)S(1)}, bf16[128,768]{1,0:T(8,128)(2,1)S(1)}, u32[]{:S(2)}, u32[]{:S(2)}) collective-permute-start(bf16[128,768]{1,0:T(8,128)(2,1)S(1)} %get-tuple-element.311), channel_id=1, source_target_pairs={{0,2},{1,3},{2,0},{3,1},{4,6},{5,7},{6,4},{7,5},{8,10},{9,11},{10,... | collective-permute-start | bytes 589832 | tf_op jit(solution)/shard_map/ppermute | solution.py:366
  956.1 37.5 %collective-permute-start.249 = (bf16[128,768]{1,0:T(8,128)(2,1)S(1)}, bf16[128,768]{1,0:T(8,128)(2,1)S(1)}, u32[]{:S(2)}, u32[]{:S(2)}) collective-permute-start(bf16[128,768]{1,0:T(8,128)(2,1)S(1)} %get-tuple-element.312), channel_id=1, source_target_pairs={{0,3},{1,2},{2,1},{3,0},{4,7},{5,6},{6,5},{7,4},{8,11},{9,10},{10,... | collective-permute-start | bytes 589832 | tf_op jit(solution)/shard_map/ppermute | solution.py:366
  957.0 39.6 %collective-permute-start.250 = (bf16[128,768]{1,0:T(8,128)(2,1)S(1)}, bf16[128,768]{1,0:T(8,128)(2,1)S(1)}, u32[]{:S(2)}, u32[]{:S(2)}) collective-permute-start(bf16[128,768]{1,0:T(8,128)(2,1)S(1)} %get-tuple-element.313), channel_id=1, source_target_pairs={{0,4},{1,5},{2,6},{3,7},{4,0},{5,1},{6,2},{7,3},{8,12},{9,13},{10,... | collective-permute-start | bytes 589832 | tf_op jit(solution)/shard_map/ppermute | solution.py:366
  985.9 37.3 %collective-permute-start.213 = (bf16[1024,512]{1,0:T(8,128)(2,1)}, bf16[1024,512]{1,0:T(8,128)(2,1)S(1)}, u32[]{:S(2)}, u32[]{:S(2)}) collective-permute-start(bf16[1024,512]{1,0:T(8,128)(2,1)} %fusion.65), channel_id=1, source_target_pairs={{0,16},{16,0},{1,17},{17,1},{2,18},{18,2},{3,19},{19,3},{4,20},{20... | collective-permute-start | bytes 3145736 | tf_op jit(solution)/shard_map/ppermute | solution.py:366
  1010.4 33.7 %collective-permute-start.201 = (bf16[320,2048]{1,0:T(8,128)(2,1)}, bf16[320,2048]{1,0:T(8,128)(2,1)}, u32[]{:S(2)}, u32[]{:S(2)}) collective-permute-start(bf16[320,2048]{1,0:T(8,128)(2,1)} %convolution_convert_fusion.2), channel_id=1, source_target_pairs={{0,8},{8,0},{1,9},{9,1},{2,10},{10,2},{3,11},{11,3},{4,12},{12,4},... | collective-permute-start | bytes 3932168 | tf_op jit(solution)/shard_map/ppermute | solution.py:366
  1020.3 57.1 %collective-permute-start.262 = (bf16[128,6144]{1,0:T(8,128)(2,1)}, bf16[128,6144]{1,0:T(8,128)(2,1)}, u32[]{:S(2)}, u32[]{:S(2)}) collective-permute-start(bf16[128,6144]{1,0:T(8,128)(2,1)} %get-tuple-element.336), channel_id=1, source_target_pairs={{0,16},{16,0},{1,17},{17,1},{2,18},{18,2},{3,19},{19,3},{4,20},{20... | collective-permute-start | bytes 4718600 | tf_op jit(solution)/shard_map/ppermute | solution.py:366
  (580 other events, 6712.1 us)

commit v2 on v1

--- a/solution.py
+++ b/solution.py
@@ -6,6 +6,7 @@
 from jax.experimental import pallas as pl
 from jax.experimental.pallas import tpu as pltpu
 from jax.sharding import PartitionSpec as P
+
 
 EPSILON = 1e-06
 MASKED = -1e30
@@ -502,7 +503,7 @@
     )(flags, *blocks)
 
 
-def place_columns(first, second, flags, widths, shared):
+def place_columns(first, second, flags, widths, shared, skip):
     count = len(first)
     rows = first[0].shape[0]
     columns = [w * count // (2 if wide else 1) for w, wide in zip(widths, shared)]
@@ -511,8 +512,8 @@
     def kernel(flags_ref, *refs):
         kept, sent = refs[2 * count :]
 
-        def fill(out, blocks):
-            left = base = 0
+        def fill(out, blocks, left):
+            base = 0
             for width, wide, room in zip(widths, shared, columns):
                 for s in range(0, count, 2 if wide else 1):
                     index = flags_ref[0] ^ s
@@ -528,13 +529,13 @@
 
         @pl.when(flags_ref[1] == 0)
         def _():
-            fill(kept, refs[:count])
-            fill(sent, refs[count : 2 * count])
+            fill(kept, refs[:count], 0)
+            fill(sent, refs[count : 2 * count], skip)
 
         @pl.when(flags_ref[1] != 0)
         def _():
-            fill(sent, refs[:count])
-            fill(kept, refs[count : 2 * count])
+            fill(sent, refs[:count], 0)
+            fill(kept, refs[count : 2 * count], skip)
 
     return pl.pallas_call(
         kernel,
@@ -719,17 +720,17 @@
             value = by_parts(parts, weights["v"][layer])
         attn, kept = attention(raw, value, layer)
         if layer == 0:
-            weights["g"] = both_layers(gate(turned["g"], attn), (ff_width,))[0]
             turned["u"] = turn(gate(sliced["u"], turned["g"]))
+            weights["g"] = both_layers(gate(turned["g"], raw), (ff_width,))[0]
             extra = None
         else:
             cotangent_rows = own_rows(cotangent)
             extra, token = gather_ring(gate(cotangent_rows, raw))
-            attn = gate(attn, token)
+            attn = gate(attn, extra[1])
         summed, token = product_scattered(attn, weights["o"][layer])
         mixed = layer_in + summed
         if layer == 0:
-            weights["u"] = both_layers(gate(turned["u"], mixed), (ff_width,))[0]
+            weights["u"] = both_layers(gate(turned["u"], token), (ff_width,))[0]
             turned["d"] = turn(gate(sliced["d"], turned["u"]))
             weights["gu"] = [
                 jnp.concatenate([weights["g"][i], weights["u"][i]], axis=1) for i in range(2)
@@ -740,9 +741,14 @@
         normed_mlp, raw_mlp = multiplied(parts, weights["gu"][layer])
         gate_raw, up_raw = raw_mlp[:, :ff_width], raw_mlp[:, ff_width:]
         activated = swiglu(gate_raw, up_raw).astype(jnp.bfloat16)
-        summed, token = product_scattered(activated, weights["d"][layer])
         stored = (layer_in, normed, kept, attn, mixed, normed_mlp, gate_raw, up_raw, activated)
-        return mixed + summed, stored, extra
+
+        def finish(after):
+            held = activated if after is None else gate(activated, after)
+            summed, _ = product_scattered(held, weights["d"][layer])
+            return ((mixed + summed).astype(jnp.bfloat16),)
+
+        return finish, stored, extra
 
     def halves(grad):
         span = grad.shape[0] // 2
@@ -763,7 +769,7 @@
         last_turn.append(turn(blocks))
         return last_turn[-1]
 
-    def backward(gathered, grad_out, stored, layer, back):
+    def backward(gathered, grad_out, stored, layer, back, late):
         layer_in, normed, kept, attn, mixed, normed_mlp, gate_raw, up_raw, activated = stored
         queries, key_raw, value, query_rot, key_rot, log_total = kept
         gain_attn, gain_mlp, gain_q, gain_k = layer_gains[layer]
@@ -775,13 +781,15 @@
         sums = {}
         sums["d"] = halves(dot_first(out_low, activated))
         sums["gu"] = halves(dot_first(normed_mlp, raw_grad))
-        back["d"] = returned(sums["d"], token)
         unused, mlp_norm_back = jax.vjp(rms_scale, mixed, gain_mlp)
         mixed_part, grad_gain_mlp = mlp_norm_back(summed)
         mixed_grad = grad_out + mixed_part
+        back["d"] = returned(sums["d"], mixed_grad)
         parts, token = gather_ring(mixed_grad.astype(jnp.bfloat16))
         branch_low, attn_grad = multiplied(parts, weights["o"][layer])
-        back["gu"] = returned(sums["gu"], parts[0])
+        if late is not None:
+            late = partial(late, attn_grad)
+        back["gu"] = returned(sums["gu"], parts[1])
         query_back, key_back, value_back = head_attend_back(
             query_rot, key_rot, value, allowed, log_total, attn_grad.astype(jnp.bfloat16)
         )
@@ -790,34 +798,44 @@
         unused, query_rope_back = jax.vjp(rope, queries, gain_q)
         query_grad, grad_gain_q = query_rope_back(query_back)
         qkv_grad = jnp.concatenate([query_grad, key_grad, value_back], axis=1).astype(jnp.bfloat16)
+        if late is not None:
+            late = late()
+            qkv_grad = gate(qkv_grad, late[0])
         summed, token = product_scattered(qkv_grad, weights["qkv"][layer])
-        grad_attn = [dot_first(normed, qkv_grad), dot_first(branch_low, attn)]
-        sums["attn"] = halves(jnp.concatenate(grad_attn, axis=1))
+        two = 2 * head_size
+        grad_vo = [dot_first(normed, qkv_grad[:, two:]), dot_first(branch_low, attn)]
+        grad_vo = jnp.concatenate(grad_vo, axis=1)
+        grad_qk = dot_first(normed, qkv_grad[:, :two])
+        if layer == 0:
+            sums = (halves(grad_qk), halves(grad_vo))
+        else:
+            sums = halves(jnp.concatenate([grad_qk, grad_vo], axis=1))
         unused, attn_norm_back = jax.vjp(rms_scale, layer_in, gain_attn)
         input_part, grad_gain_attn = attn_norm_back(summed)
         small = (grad_gain_attn, grad_gain_mlp, grad_gain_q, grad_gain_k)
-        points = (mixed_grad, branch_low, qkv_grad)
-        return mixed_grad + input_part, sums["attn"], small, points
-
-    out_first, stored_first, _ = forward(own_rows(inputs).astype(jnp.float32), 0)
-    out_first = out_first.astype(jnp.bfloat16)
+        points = (branch_low, token)
+        return mixed_grad + input_part, sums, small, points, late
+
+    finish, stored_first, _ = forward(own_rows(inputs).astype(jnp.float32), 0)
+    out_first = finish(None)[0]
     weights["qkv"] = [
         jnp.concatenate([weights["qk"][i], weights["v"][i]], axis=1) for i in range(2)
     ]
-    out_second, stored_second, gathered = forward(out_first.astype(jnp.float32), 1)
-    out_second = out_second.astype(jnp.bfloat16)
+    finish, stored_second, gathered = forward(out_first.astype(jnp.float32), 1)
     back_second, back_first = {}, {}
-    grad_second, late, small_second, points = backward(
-        gathered, own_rows(cotangent).astype(jnp.float32), stored_second, 1, back_second
-    )
+    grad_second, waiting, small_second, points, last = backward(
+        gathered, own_rows(cotangent).astype(jnp.float32), stored_second, 1, back_second, finish
+    )
+    out_second = last[0]
     grad_second = grad_second.astype(jnp.bfloat16)
-    gathered, token = gather_ring(grad_second)
-    back_second["attn"] = returned(late, token)
-    grad_first, late, small_first, points = backward(
-        gathered, grad_second.astype(jnp.float32), stored_first, 0, back_first
+    gathered, _ = gather_ring(grad_second)
+    back_second["attn"] = returned(waiting, gathered[1])
+    grad_first, waiting, small_first, points, last = backward(
+        gathered, grad_second.astype(jnp.float32), stored_first, 0, back_first, None
     )
     grad_first = grad_first.astype(jnp.bfloat16)
-    back_first["attn"] = returned(late, None)
+    back_first["qk"] = returned(waiting[0], None)
+    back_first["vo"] = returned(waiting[1], None)
 
     def by_section(first, second):
         first, second = unhalved(first), unhalved(second)
@@ -834,9 +852,10 @@
     section_out = by_section(out_first, out_second)
     input_grads = by_section(grad_first, grad_second)
 
-    def owned(name, widths, shared, token):
+    def owned(name, widths, shared, token, other=None, skip=0):
         firsts = back_first[name] if token is None else gate(back_first[name], token)
-        kept, sent = place_columns(firsts, back_second[name], flags, widths, shared)
+        seconds = back_second[other or name]
+        kept, sent = place_columns(firsts, seconds, flags, widths, shared, skip)
         taken = paired(sent, "section", 1)
         both = jnp.where(
             plane == 0,
@@ -845,15 +864,16 @@
         )
         return both.astype(jnp.float32)
 
-    _, branch_point, summed_point = points
+    branch_point, summed_point = points
     ff_total = w_gate.shape[2]
     grad_d = owned("d", (ff_width,), (False,), branch_point)
     grad_gu = owned("gu", (ff_width,) * 2, (False,) * 2, summed_point)
-    grad_attn = owned("attn", (head_size,) * 4, (False, True, True, False), None)
-    edges = [0]
-    for array in (w_query, key_weight, value_weight, w_output):
-        edges.append(edges[-1] + array.shape[2])
-    attn_grads = [grad_attn[:, a:b] for a, b in zip(edges, edges[1:])]
+    grad_qk = owned("qk", (head_size,) * 2, (False, True), None, "attn")
+    grad_vo = owned("vo", (head_size,) * 2, (True, False), None, "attn", 2 * head_size)
+    q_total, v_total = w_query.shape[2], value_weight.shape[2]
+    attn_grads = (
+        grad_qk[:, :q_total], grad_qk[:, q_total:], grad_vo[:, :v_total], grad_vo[:, v_total:],
+    )
     mlp_grads = (grad_gu[:, :ff_total], grad_gu[:, ff_total:], grad_d)
 
     rows_of = jnp.concatenate(
@@ -870,12 +890,15 @@
         axis=1,
     )
 
-    def row(to):
-        return lax.dynamic_index_in_dim(rows_of, to, 0, keepdims=False)
-
-    gain_sum = row(me)
-    for s in range(1, count):
-        gain_sum = gain_sum + paired(row(me ^ s), "dp", s)
+    gain_sum, step = rows_of, count // 2
+    while step:
+        bit = (me // step) % 2
+        gain_sum = gain_sum.reshape(2, step, -1)
+        kept = lax.dynamic_index_in_dim(gain_sum, bit, 0, keepdims=False)
+        sent = lax.dynamic_index_in_dim(gain_sum, 1 - bit, 0, keepdims=False)
+        gain_sum = kept + paired(sent, "dp", step)
+        step //= 2
+    gain_sum = gain_sum.reshape(-1)
     gain_sum = gain_sum + paired(gain_sum, "tensor", 1)
     gain_sum = gain_sum + paired(gain_sum, "section", 1)
     mine = jnp.where(plane == 0, gain_sum[:per_layer], gain_sum[per_layer:])

time: 1130 us -> 1210 us (1.071)
  waiting for transfers between devices: 439 us -> 484 us
  starting transfers between devices: 324 us -> 357 us
    ppermute x161 -> x166, waiting for transfers between devices: 204 us -> 248 us  [paired(): return lax.ppermute(x, axis, [(i, i ^ flip) for i in range(count)])]
    ppermute x112, starting transfers between devices: 129 us -> 164 us  [ring(): return lax.ppermute(x, ('tensor', 'dp'), pairs)]
    unnamed x675 -> x655, local copies, waits for them, and re-layouts: 24.7 us -> 21.2 us
    dot_general x12 -> x14, matrix products: 31.5 us -> 34.3 us  [dot_first(): lax.dot_general(left, right, (((0,), (0,)), ((), ())), preferred_element_...]
    ppermute x161 -> x166, starting transfers between devices: 194 us -> 192 us  [paired(): return lax.ppermute(x, axis, [(i, i ^ flip) for i in range(count)])]
  transfers between devices with their start and end apart: 273 -> 278, of which waited for: 119 -> 119; matrix products, arithmetic and copies ran while one was open for 19% -> 18% of each run, Pallas kernels for 5% -> 5%
where the time goes in v2:
time: 1210 us; the launch traced here: 1200 us
  waiting for transfers between devices  484 us (40%)
  starting transfers between devices  357 us (30%)
  matrix products  124 us (10%)
  other arithmetic  105 us (9%)
  Pallas kernels  70.5 us (6%)
  local copies, waits for them, and re-layouts  56.5 us (5%)
    ppermute x166, waiting for transfers between devices, paired(): return lax.ppermute(x, axis, [(i, i ^ flip) for i in range(count)])  248 us
    ppermute x112, waiting for transfers between devices, ring(): return lax.ppermute(x, ('tensor', 'dp'), pairs)  236 us
    ppermute x166, starting transfers between devices, paired(): return lax.ppermute(x, axis, [(i, i ^ flip) for i in range(count)])  192 us
    ppermute x112, starting transfers between devices, ring(): return lax.ppermute(x, ('tensor', 'dp'), pairs)  164 us
    dot_general x37, matrix products, dot_plain(): return jnp.dot(left, right, preferred_element_type=jnp.float32)  52.8 us
    pallas_call x17, Pallas kernels, joined(): pl.pallas_call(kernel, out_shape=jax.ShapeDtypeStruct((rows, width), piec...  40.9 us
    dot_general x28, matrix products, dot_last(): lax.dot_general(left, right, (((1,), (1,)), ((), ())), preferred_element_...  36.8 us
    dot_general x14, matrix products, dot_first(): lax.dot_general(left, right, (((0,), (0,)), ((), ())), preferred_element_...  34.3 us
  transfers between devices with their start and end apart: 278, of which 119 were waited for; matrix products, arithmetic and copies ran while one was open for 18% of the time, Pallas kernels for 5%

profile of v2, /device:TPU:0, one launch (start us, length us, event | category | flops | bytes accessed | tf_op | source)
XLA Modules:
  0.0 1202.1 jit_solution(8564572933384620973)
XLA Ops:
  26.3 7.8 collective-permute-done.22.refs_5_
  105.6 13.6 %collective-permute-done.33 = bf16[2048,128]{1,0:T(8,128)(2,1)} collective-permute-done((bf16[2048,128]{1,0:T(8,128)(2,1)S(1)}, bf16[2048,128]{1,0:T(8,128)(2,1)}, u32[]{:S(2)}, u32[]{:S(2)}) %collective-permute-start.33) | collective-permute-done | bytes 524320 | tf_op jit(solution)/shard_map/ppermute | solution.py:367
  156.4 8.6 collective-permute-done.37
  210.0 13.3 %collective-permute-done.55.refs_5_ = bf16[256,384]{1,0:T(8,128)(2,1)S(1)} collective-permute-done((bf16[256,384]{1,0:T(8,128)(2,1)S(1)}, bf16[256,384]{1,0:T(8,128)(2,1)S(1)}, u32[]{:S(2)}, u32[]{:S(2)}) %collective-permute-start.55) | collective-permute-done | bytes 196640 | tf_op jit(solution)/shard_map/ppermute | solution.py:367
  225.8 6.9 collective-permute-start.60
  248.2 13.0 %collective-permute-done.62.refs_4_ = bf16[256,384]{1,0:T(8,128)(2,1)} collective-permute-done((bf16[256,384]{1,0:T(8,128)(2,1)}, bf16[256,384]{1,0:T(8,128)(2,1)}, u32[]{:S(2)}, u32[]{:S(2)}) %collective-permute-start.62) | collective-permute-done | bytes 196640 | tf_op jit(solution)/shard_map/ppermute | solution.py:367
  268.0 8.1 collective-permute-start.47
  325.2 7.7 collective-permute-done.75.refs_5_
  345.7 18.9 %collective-permute-done.78 = bf16[2048,384]{1,0:T(8,128)(2,1)S(1)} collective-permute-done((bf16[2048,384]{1,0:T(8,128)(2,1)}, bf16[2048,384]{1,0:T(8,128)(2,1)S(1)}, u32[]{:S(2)}, u32[]{:S(2)}) %collective-permute-start.78) | collective-permute-done | bytes 1572896 | tf_op jit(solution)/shard_map/ppermute | solution.py:367
  368.5 8.0 collective-permute-start.81
  376.5 6.1 collective-permute-done.81
  500.4 6.4 collective-permute-done.109
  520.7 6.4 collective-permute-done.114
  655.8 5.8 collective-permute-done.143.refs_4_
  695.3 6.2 collective-permute-done.163
  715.0 6.2 collective-permute-done.168
  868.2 13.3 %collective-permute-done.229.refs_12_ = bf16[128,768]{1,0:T(8,128)(2,1)S(1)} collective-permute-done((bf16[128,768]{1,0:T(8,128)(2,1)S(1)}, bf16[128,768]{1,0:T(8,128)(2,1)S(1)}, u32[]{:S(2)}, u32[]{:S(2)}) %collective-permute-start.229) | collective-permute-done | bytes 196640 | tf_op jit(solution)/shard_map/ppermute | solution.py:367
  909.6 25.1 %collective-permute-done.215 = bf16[1024,384]{1,0:T(8,128)(2,1)S(1)} collective-permute-done((bf16[1024,384]{1,0:T(8,128)(2,1)S(1)}, bf16[1024,384]{1,0:T(8,128)(2,1)S(1)}, u32[]{:S(2)}, u32[]{:S(2)}) %collective-permute-start.215) | collective-permute-done | bytes 786464 | tf_op jit(solution)/shard_map/ppermute | solution.py:367
  936.5 10.0 collective-permute-done.236.refs_12_
  955.8 6.0 collective-permute-done.239.refs_15_
  1012.4 6.6 pad_maximum_fusion.2
  1039.1 16.7 %collective-permute-done.250.refs_4_ = bf16[128,768]{1,0:T(8,128)(2,1)S(1)} collective-permute-done((bf16[128,768]{1,0:T(8,128)(2,1)S(1)}, bf16[128,768]{1,0:T(8,128)(2,1)S(1)}, u32[]{:S(2)}, u32[]{:S(2)}) %collective-permute-start.250) | collective-permute-done | bytes 196640 | tf_op jit(solution)/shard_map/ppermute | solution.py:367
  1062.3 8.1 collective-permute-start.255
  1165.2 26.8 %collective-permute-done.277 = f32[1536]{0:T(1024)S(1)} collective-permute-done((f32[1536]{0:T(1024)S(1)}, f32[1536]{0:T(1024)S(1)}, u32[]{:S(2)}, u32[]{:S(2)}) %collective-permute-start.277) | collective-permute-done | bytes 6176 | tf_op jit(solution)/shard_map/ppermute | solution.py:367
  (1543 shorter events, 940.5 us)
Async XLA Ops:
  88.4 32.8 %collective-permute-start.25 = (bf16[2048,256]{1,0:T(8,128)(2,1)}, bf16[2048,256]{1,0:T(8,128)(2,1)}, u32[]{:S(2)}, u32[]{:S(2)}) collective-permute-start(bf16[2048,256]{1,0:T(8,128)(2,1)} %shard_map.240), channel_id=1, source_target_pairs={{0,16},{16,0},{1,17},{17,1},{2,18},{18,2},{3,19},{19,3},{4,20},{20... | collective-permute-start | bytes 3145736 | tf_op jit(solution)/shard_map/ppermute | solution.py:367
  196.1 39.4 %collective-permute-start.40 = (bf16[64,2048]{1,0:T(8,128)(2,1)S(1)}, bf16[64,2048]{1,0:T(8,128)(2,1)S(1)}, u32[]{:S(2)}, u32[]{:S(2)}) collective-permute-start(bf16[64,2048]{1,0:T(8,128)(2,1)S(1)} %get-tuple-element.433), channel_id=1, source_target_pairs={{0,1},{2,0},{4,2},{6,4},{7,6},{5,7},{3,5},{1,3},{8,10},{10,12},{12... | collective-permute-start | bytes 786440 | tf_op jit(solution)/shard_map/ppermute | solution.py:381
  197.4 41.6 %collective-permute-start.44 = (bf16[64,2048]{1,0:T(8,128)(2,1)}, bf16[64,2048]{1,0:T(8,128)(2,1)S(1)}, u32[]{:S(2)}, u32[]{:S(2)}) collective-permute-start(bf16[64,2048]{1,0:T(8,128)(2,1)} %collective-permute-done.43), channel_id=1, source_target_pairs={{0,8},{8,0},{1,9},{9,1},{2,10},{10,2},{3,11},{11,3},{4,12},{12,4},... | collective-permute-start | bytes 786440 | tf_op jit(solution)/shard_map/ppermute | solution.py:367
  239.0 55.5 %collective-permute-start.58 = (bf16[2048,384]{1,0:T(8,128)(2,1)}, bf16[2048,384]{1,0:T(8,128)(2,1)S(1)}, u32[]{:S(2)}, u32[]{:S(2)}) collective-permute-start(bf16[2048,384]{1,0:T(8,128)(2,1)} %shard_map.243), channel_id=1, source_target_pairs={{0,16},{16,0},{1,17},{17,1},{2,18},{18,2},{3,19},{19,3},{4,20},{20... | collective-permute-start | bytes 4718600 | tf_op jit(solution)/shard_map/ppermute | solution.py:367
  267.9 53.4 %collective-permute-start.66 = (bf16[2048,384]{1,0:T(8,128)(2,1)}, bf16[2048,384]{1,0:T(8,128)(2,1)}, u32[]{:S(2)}, u32[]{:S(2)}) collective-permute-start(bf16[2048,384]{1,0:T(8,128)(2,1)} %shard_map.244), channel_id=1, source_target_pairs={{0,16},{16,0},{1,17},{17,1},{2,18},{18,2},{3,19},{19,3},{4,20},{20... | collective-permute-start | bytes 4718600 | tf_op jit(solution)/shard_map/ppermute | solution.py:367
  536.2 39.0 %collective-permute-start.127 = (bf16[320,2048]{1,0:T(8,128)(2,1)}, bf16[320,2048]{1,0:T(8,128)(2,1)}, u32[]{:S(2)}, u32[]{:S(2)}) collective-permute-start(bf16[320,2048]{1,0:T(8,128)(2,1)} %shard_map.252), channel_id=1, source_target_pairs={{0,8},{8,0},{1,9},{9,1},{2,10},{10,2},{3,11},{11,3},{4,12},{12,4},... | collective-permute-start | bytes 3932168 | tf_op jit(solution)/shard_map/ppermute | solution.py:367
  594.1 34.7 %collective-permute-start.149 = (bf16[320,2048]{1,0:T(8,128)(2,1)S(1)}, bf16[320,2048]{1,0:T(8,128)(2,1)S(1)}, u32[]{:S(2)}, u32[]{:S(2)}) collective-permute-start(bf16[320,2048]{1,0:T(8,128)(2,1)S(1)} %convolution_convert_fusion.5), channel_id=1, source_target_pairs={{0,8},{8,0},{1,9},{9,1},{2,10},{10,2},{3,11},{11,3},{4,12},{12,4},... | collective-permute-start | bytes 3932168 | tf_op jit(solution)/shard_map/ppermute | solution.py:367
  748.5 56.3 %collective-permute-start.217 = (bf16[1024,768]{1,0:T(8,128)(2,1)}, bf16[1024,768]{1,0:T(8,128)(2,1)}, u32[]{:S(2)}, u32[]{:S(2)}) collective-permute-start(bf16[1024,768]{1,0:T(8,128)(2,1)} %dynamic-slice_convert_fusion), channel_id=1, source_target_pairs={{0,16},{16,0},{1,17},{17,1},{2,18},{18,2},{3,19},{19,3},{4,20},{20... | collective-permute-start | bytes 4718600 | tf_op jit(solution)/shard_map/ppermute | solution.py:367
  801.8 33.2 %collective-permute-start.216 = (bf16[1024,512]{1,0:T(8,128)(2,1)S(1)}, bf16[1024,512]{1,0:T(8,128)(2,1)S(1)}, u32[]{:S(2)}, u32[]{:S(2)}) collective-permute-start(bf16[1024,512]{1,0:T(8,128)(2,1)S(1)} %dynamic-slice_convert_fusion.2), channel_id=1, source_target_pairs={{0,16},{16,0},{1,17},{17,1},{2,18},{18,2},{3,19},{19,3},{4,20},{20... | collective-permute-start | bytes 3145736 | tf_op jit(solution)/shard_map/ppermute | solution.py:367
  828.2 35.1 %collective-permute-start.226 = (bf16[128,768]{1,0:T(8,128)(2,1)S(1)}, bf16[128,768]{1,0:T(8,128)(2,1)S(1)}, u32[]{:S(2)}, u32[]{:S(2)}) collective-permute-start(bf16[128,768]{1,0:T(8,128)(2,1)S(1)} %get-tuple-element.300), channel_id=1, source_target_pairs={{0,1},{1,0},{2,3},{3,2},{4,5},{5,4},{6,7},{7,6},{8,9},{9,8},{10,11... | collective-permute-start | bytes 589832 | tf_op jit(solution)/shard_map/ppermute | solution.py:367
  829.7 33.7 %collective-permute-start.227 = (bf16[128,768]{1,0:T(8,128)(2,1)S(1)}, bf16[128,768]{1,0:T(8,128)(2,1)S(1)}, u32[]{:S(2)}, u32[]{:S(2)}) collective-permute-start(bf16[128,768]{1,0:T(8,128)(2,1)S(1)} %get-tuple-element.301), channel_id=1, source_target_pairs={{0,2},{1,3},{2,0},{3,1},{4,6},{5,7},{6,4},{7,5},{8,10},{9,11},{10,... | collective-permute-start | bytes 589832 | tf_op jit(solution)/shard_map/ppermute | solution.py:367
  835.0 32.3 %collective-permute-start.228 = (bf16[128,768]{1,0:T(8,128)(2,1)S(1)}, bf16[128,768]{1,0:T(8,128)(2,1)S(1)}, u32[]{:S(2)}, u32[]{:S(2)}) collective-permute-start(bf16[128,768]{1,0:T(8,128)(2,1)S(1)} %get-tuple-element.302), channel_id=1, source_target_pairs={{0,3},{1,2},{2,1},{3,0},{4,7},{5,6},{6,5},{7,4},{8,11},{9,10},{10,... | collective-permute-start | bytes 589832 | tf_op jit(solution)/shard_map/ppermute | solution.py:367
  881.4 86.0 %collective-permute-start.214 = (bf16[1024,768]{1,0:T(8,128)(2,1)}, bf16[1024,768]{1,0:T(8,128)(2,1)}, u32[]{:S(2)}, u32[]{:S(2)}) collective-permute-start(bf16[1024,768]{1,0:T(8,128)(2,1)} %dynamic-slice_convert_fusion.1), channel_id=1, source_target_pairs={{0,16},{16,0},{1,17},{17,1},{2,18},{18,2},{3,19},{19,3},{4,20},{20... | collective-permute-start | bytes 4718600 | tf_op jit(solution)/shard_map/ppermute | solution.py:367
  886.6 48.1 %collective-permute-start.215 = (bf16[1024,384]{1,0:T(8,128)(2,1)S(1)}, bf16[1024,384]{1,0:T(8,128)(2,1)S(1)}, u32[]{:S(2)}, u32[]{:S(2)}) collective-permute-start(bf16[1024,384]{1,0:T(8,128)(2,1)S(1)} %dynamic-slice_convert_fusion.4), channel_id=1, source_target_pairs={{0,16},{16,0},{1,17},{17,1},{2,18},{18,2},{3,19},{19,3},{4,20},{20... | collective-permute-start | bytes 2359304 | tf_op jit(solution)/shard_map/ppermute | solution.py:367
  901.7 46.0 %collective-permute-start.196 = (bf16[64,2048]{1,0:T(8,128)(2,1)}, bf16[64,2048]{1,0:T(8,128)(2,1)}, u32[]{:S(2)}, u32[]{:S(2)}) collective-permute-start(bf16[64,2048]{1,0:T(8,128)(2,1)} %collective-permute-done.194.refs_3_), channel_id=1, source_target_pairs={{0,2},{2,4},{4,6},{6,7},{7,5},{5,3},{3,1},{1,0},{8,9},{10,8},{12,1... | collective-permute-start | bytes 786440 | tf_op jit(solution)/shard_map/ppermute | solution.py:381
  905.9 41.8 %collective-permute-start.195 = (bf16[64,2048]{1,0:T(8,128)(2,1)}, bf16[64,2048]{1,0:T(8,128)(2,1)}, u32[]{:S(2)}, u32[]{:S(2)}) collective-permute-start(bf16[64,2048]{1,0:T(8,128)(2,1)} %collective-permute-done.193.refs_2_), channel_id=1, source_target_pairs={{0,2},{2,4},{4,6},{6,7},{7,5},{5,3},{3,1},{1,0},{8,9},{10,8},{12,1... | collective-permute-start | bytes 786440 | tf_op jit(solution)/shard_map/ppermute | solution.py:381
  954.9 37.9 %collective-permute-start.199 = (bf16[320,2048]{1,0:T(8,128)(2,1)}, bf16[320,2048]{1,0:T(8,128)(2,1)}, u32[]{:S(2)}, u32[]{:S(2)}) collective-permute-start(bf16[320,2048]{1,0:T(8,128)(2,1)} %shard_map.257), channel_id=1, source_target_pairs={{0,8},{8,0},{1,9},{9,1},{2,10},{10,2},{3,11},{11,3},{4,12},{12,4},... | collective-permute-start | bytes 3932168 | tf_op jit(solution)/shard_map/ppermute | solution.py:367
  985.8 44.4 %collective-permute-start.247 = (bf16[128,768]{1,0:T(8,128)(2,1)}, bf16[128,768]{1,0:T(8,128)(2,1)}, u32[]{:S(2)}, u32[]{:S(2)}) collective-permute-start(bf16[128,768]{1,0:T(8,128)(2,1)} %get-tuple-element.324), channel_id=1, source_target_pairs={{0,1},{1,0},{2,3},{3,2},{4,5},{5,4},{6,7},{7,6},{8,9},{9,8},{10,11... | collective-permute-start | bytes 589832 | tf_op jit(solution)/shard_map/ppermute | solution.py:367
  987.1 45.8 %collective-permute-start.248 = (bf16[128,768]{1,0:T(8,128)(2,1)}, bf16[128,768]{1,0:T(8,128)(2,1)}, u32[]{:S(2)}, u32[]{:S(2)}) collective-permute-start(bf16[128,768]{1,0:T(8,128)(2,1)} %get-tuple-element.325), channel_id=1, source_target_pairs={{0,2},{1,3},{2,0},{3,1},{4,6},{5,7},{6,4},{7,5},{8,10},{9,11},{10,... | collective-permute-start | bytes 589832 | tf_op jit(solution)/shard_map/ppermute | solution.py:367
  991.7 42.4 %collective-permute-start.249 = (bf16[128,768]{1,0:T(8,128)(2,1)}, bf16[128,768]{1,0:T(8,128)(2,1)}, u32[]{:S(2)}, u32[]{:S(2)}) collective-permute-start(bf16[128,768]{1,0:T(8,128)(2,1)} %get-tuple-element.326), channel_id=1, source_target_pairs={{0,3},{1,2},{2,1},{3,0},{4,7},{5,6},{6,5},{7,4},{8,11},{9,10},{10,... | collective-permute-start | bytes 589832 | tf_op jit(solution)/shard_map/ppermute | solution.py:367
  1010.2 60.1 %collective-permute-start.202 = (bf16[192,2048]{1,0:T(8,128)(2,1)}, bf16[192,2048]{1,0:T(8,128)(2,1)}, u32[]{:S(2)}, u32[]{:S(2)}) collective-permute-start(bf16[192,2048]{1,0:T(8,128)(2,1)} %convolution_convert_fusion.12), channel_id=1, source_target_pairs={{0,8},{8,0},{1,9},{9,1},{2,10},{10,2},{3,11},{11,3},{4,12},{12,4},... | collective-permute-start | bytes 2359304 | tf_op jit(solution)/shard_map/ppermute | solution.py:367
  1060.8 57.0 %collective-permute-start.201 = (bf16[320,2048]{1,0:T(8,128)(2,1)}, bf16[320,2048]{1,0:T(8,128)(2,1)}, u32[]{:S(2)}, u32[]{:S(2)}) collective-permute-start(bf16[320,2048]{1,0:T(8,128)(2,1)} %convolution_convert_fusion.2), channel_id=1, source_target_pairs={{0,8},{8,0},{1,9},{9,1},{2,10},{10,2},{3,11},{11,3},{4,12},{12,4},... | collective-permute-start | bytes 3932168 | tf_op jit(solution)/shard_map/ppermute | solution.py:367
  1155.8 39.2 %collective-permute-start.271 = (bf16[128,6144]{1,0:T(8,128)(2,1)}, bf16[128,6144]{1,0:T(8,128)(2,1)}, u32[]{:S(2)}, u32[]{:S(2)}) collective-permute-start(bf16[128,6144]{1,0:T(8,128)(2,1)} %get-tuple-element.360), channel_id=1, source_target_pairs={{0,16},{16,0},{1,17},{17,1},{2,18},{18,2},{3,19},{19,3},{4,20},{20... | collective-permute-start | bytes 4718600 | tf_op jit(solution)/shard_map/ppermute | solution.py:367
  1163.3 31.4 %collective-permute-start.211 = (bf16[64,2048]{1,0:T(8,128)(2,1)S(1)}, bf16[64,2048]{1,0:T(8,128)(2,1)S(1)}, u32[]{:S(2)}, u32[]{:S(2)}) collective-permute-start(bf16[64,2048]{1,0:T(8,128)(2,1)S(1)} %select_n.876), channel_id=1, source_target_pairs={{0,16},{16,0},{1,17},{17,1},{2,18},{18,2},{3,19},{19,3},{4,20},{20... | collective-permute-start | bytes 786440 | tf_op jit(solution)/shard_map/ppermute | solution.py:367
  (575 other events, 6956.3 us)

commit v3 on v2

--- a/solution.py
+++ b/solution.py
@@ -8,6 +8,7 @@
 from jax.sharding import PartitionSpec as P
 
 
+SECTION, TENSOR, DP = "section", "tensor", "dp"
 EPSILON = 1e-06
 MASKED = -1e30
 
@@ -140,17 +141,17 @@
     query_gain,
     key_gain,
 ):
-    section_first = lax.axis_index("section") == 0
+    section_first = lax.axis_index(SECTION) == 0
     gathered = (
-        lax.all_gather(w_query[0], "dp", axis=0, tiled=True),
-        lax.all_gather(key_weight[0], "dp", axis=0, tiled=True),
-        lax.all_gather(value_weight[0], "dp", axis=0, tiled=True),
-        lax.all_gather(w_output[0], "dp", axis=0, tiled=True),
-        lax.all_gather(w_gate[0], "dp", axis=0, tiled=True),
-        lax.all_gather(w_up[0], "dp", axis=0, tiled=True),
-        lax.all_gather(w_down[0], "dp", axis=0, tiled=True),
-        lax.all_gather(attn_gain[0], "dp", axis=0, tiled=True),
-        lax.all_gather(mlp_gain[0], "dp", axis=0, tiled=True),
+        lax.all_gather(w_query[0], DP, axis=0, tiled=True),
+        lax.all_gather(key_weight[0], DP, axis=0, tiled=True),
+        lax.all_gather(value_weight[0], DP, axis=0, tiled=True),
+        lax.all_gather(w_output[0], DP, axis=0, tiled=True),
+        lax.all_gather(w_gate[0], DP, axis=0, tiled=True),
+        lax.all_gather(w_up[0], DP, axis=0, tiled=True),
+        lax.all_gather(w_down[0], DP, axis=0, tiled=True),
+        lax.all_gather(attn_gain[0], DP, axis=0, tiled=True),
+        lax.all_gather(mlp_gain[0], DP, axis=0, tiled=True),
     )
     w_q, w_k, w_v, w_o, w_g, w_u, w_d = gathered[:7]
     gain_attn = gathered[7].astype(jnp.float32)
@@ -158,10 +159,10 @@
     gain_q = query_gain[0].astype(jnp.float32)
     gain_k = key_gain[0].astype(jnp.float32)
     head_size = gain_q.shape[0]
-    doc_table = lax.all_gather(segments, "dp", axis=1, tiled=True)
+    doc_table = lax.all_gather(segments, DP, axis=1, tiled=True)
     batch_count, row_count, model_width = inputs.shape
     token_count = doc_table.shape[1]
-    positions = lax.axis_index("dp") * row_count + jnp.arange(row_count, dtype=jnp.int32)
+    positions = lax.axis_index(DP) * row_count + jnp.arange(row_count, dtype=jnp.int32)
     key_pos = jnp.arange(token_count, dtype=jnp.int32)
     cosine, sine_table = rope_tables(positions, head_size)
     rope_query = partial(rotate_norm, cosine=cosine, sine_table=sine_table)
@@ -181,20 +182,20 @@
         forward_value_raw = dot_plain(forward_normed, w_v).astype(jnp.bfloat16)
         forward_query_rot = rope_query(forward_queries, gain_q).astype(jnp.bfloat16)
         forward_key_rot = rope_query(forward_key_raw, gain_k).astype(jnp.bfloat16)
-        forward_keys_all = lax.all_gather(forward_key_rot, "dp", axis=0, tiled=True)
-        forward_values_all = lax.all_gather(forward_value_raw, "dp", axis=0, tiled=True)
+        forward_keys_all = lax.all_gather(forward_key_rot, DP, axis=0, tiled=True)
+        forward_values_all = lax.all_gather(forward_value_raw, DP, axis=0, tiled=True)
         forward_allowed = (key_pos[None, :] <= positions[:, None]) & (
             own_segs[:, None] == doc_row[None, :]
         )
         forward_attn, forward_log_total = attend(
             forward_query_rot, forward_keys_all, forward_values_all, forward_allowed, head_size
         )
-        forward_mixed = layer_in + lax.psum(dot_last(forward_attn, w_o), "tensor")
+        forward_mixed = layer_in + lax.psum(dot_last(forward_attn, w_o), TENSOR)
         forward_normed_mlp = rms_scale(forward_mixed, gain_mlp).astype(jnp.bfloat16)
         forward_gate_raw = dot_plain(forward_normed_mlp, w_g)
         forward_up_raw = dot_plain(forward_normed_mlp, w_u)
         forward_activated = swiglu(forward_gate_raw, forward_up_raw).astype(jnp.bfloat16)
-        layer_out = forward_mixed + lax.psum(dot_last(forward_activated, w_d), "tensor")
+        layer_out = forward_mixed + lax.psum(dot_last(forward_activated, w_d), TENSOR)
         forward_stored = (
             layer_in,
             forward_normed,
@@ -217,7 +218,7 @@
         stored_steps.append(stored)
         outgoing_steps.append(outgoing)
         if step_index < batch_count:
-            arrived = shifted(outgoing, "section", 1)
+            arrived = shifted(outgoing, SECTION, 1)
     section_out = jnp.stack(
         [
             jnp.where(section_first, outgoing_steps[batch_index], outgoing_steps[batch_index + 1])
@@ -266,8 +267,8 @@
             activated,
             allowed,
         ) = stored[:15]
-        keys_all = lax.all_gather(key_rot, "dp", axis=0, tiled=True)
-        values_all = lax.all_gather(value_raw, "dp", axis=0, tiled=True)
+        keys_all = lax.all_gather(key_rot, DP, axis=0, tiled=True)
+        values_all = lax.all_gather(value_raw, DP, axis=0, tiled=True)
         mlp_grad = grad_out.astype(jnp.bfloat16)
         act_grad = dot_plain(mlp_grad, w_d)
         grad_wd = dot_first(mlp_grad, activated)
@@ -278,7 +279,7 @@
         grad_wg = dot_first(normed_mlp, gate_grad)
         grad_wu = dot_first(normed_mlp, up_grad)
         normed_mlp_grad = lax.psum(
-            (dot_last(gate_grad, w_g) + dot_last(up_grad, w_u)).astype(jnp.bfloat16), "tensor"
+            (dot_last(gate_grad, w_g) + dot_last(up_grad, w_u)).astype(jnp.bfloat16), TENSOR
         ).astype(jnp.float32)
         unused, mlp_norm_back = jax.vjp(rms_scale, mixed, gain_mlp)
         mixed_part, grad_gain_mlp = mlp_norm_back(normed_mlp_grad)
@@ -290,10 +291,10 @@
             query_rot, keys_all, values_all, allowed, log_total, attn_grad, head_size
         )
         backward_key_total = lax.psum_scatter(
-            key_back.astype(jnp.bfloat16), "dp", scatter_dimension=0, tiled=True
+            key_back.astype(jnp.bfloat16), DP, scatter_dimension=0, tiled=True
         ).astype(jnp.float32)
         value_total = lax.psum_scatter(
-            value_back.astype(jnp.bfloat16), "dp", scatter_dimension=0, tiled=True
+            value_back.astype(jnp.bfloat16), DP, scatter_dimension=0, tiled=True
         )
         unused, key_rope_back = jax.vjp(rope_query, key_raw, gain_k)
         key_gradient, grad_gain_k = key_rope_back(backward_key_total)
@@ -308,7 +309,7 @@
             (
                 dot_last(query_grad, w_q) + dot_last(key_gradient, w_k) + dot_last(value_total, w_v)
             ).astype(jnp.bfloat16),
-            "tensor",
+            TENSOR,
         ).astype(jnp.float32)
         unused, attn_norm_back = jax.vjp(rms_scale, backward_layer_in, gain_attn)
         input_part, grad_gain_attn = attn_norm_back(normed_grad)
@@ -331,7 +332,7 @@
         outgoing = input_grad.astype(jnp.bfloat16)
         grad_steps.append(outgoing)
         if step_index < batch_count:
-            back_arrived = shifted(outgoing, "section", -1)
+            back_arrived = shifted(outgoing, SECTION, -1)
         totals = (
             weight_part if totals is None else tuple((a + b for a, b in zip(totals, weight_part)))
         )
@@ -342,9 +343,9 @@
         )
     shards = jax.tree.map(
         lambda part: part.astype(jnp.float32),
-        lax.psum_scatter(as_sent(totals), "dp", scatter_dimension=0, tiled=True),
-    )
-    query_total, key_total = lax.psum(norm_totals, ("tensor", "dp"))
+        lax.psum_scatter(as_sent(totals), DP, scatter_dimension=0, tiled=True),
+    )
+    query_total, key_total = lax.psum(norm_totals, (TENSOR, DP))
     input_grads = jnp.stack(
         [
             jnp.where(
@@ -372,13 +373,13 @@
 
 
 def ring(x, by):
-    order = ring_order(lax.axis_size("dp"))
+    order = ring_order(lax.axis_size(DP))
     count = len(order)
     pairs = []
     for core, step in ((0, by), (1, -by)):
         for i in range(count):
             pairs.append((core * count + order[i], core * count + order[(i + step) % count]))
-    return lax.ppermute(x, ("tensor", "dp"), pairs)
+    return lax.ppermute(x, (TENSOR, DP), pairs)
 
 
 def received_order(count):
@@ -418,9 +419,9 @@
 
 
 def gather_ring(chunk):
-    count = lax.axis_size("dp")
+    count = lax.axis_size(DP)
     half = count // 2
-    lead, lag = chunk, paired(chunk, "tensor", 1)
+    lead, lag = chunk, paired(chunk, TENSOR, 1)
     chunks, token = [chunk], None
     for step in range(1, half + 1):
         lead = ring(lead, 1)
@@ -432,7 +433,7 @@
             token = lead
     cut = near_chunks(count)
     near, far = joined(gate(chunks[:cut], token)), joined(chunks[cut:])
-    return [near, far, paired(near, "tensor", 1), paired(far, "tensor", 1)], token
+    return [near, far, paired(near, TENSOR, 1), paired(far, TENSOR, 1)], token
 
 
 def multiplied(parts, weight):
@@ -444,7 +445,7 @@
 
 
 def product_scattered(act, weight):
-    count = lax.axis_size("dp")
+    count = lax.axis_size(DP)
     half = count // 2
     side = act.shape[0] // 2
     rows = side // count
@@ -452,8 +453,8 @@
     far_sum = dot_last(act[side + near :], weight).astype(jnp.bfloat16)
     near_sum = dot_last(act[side : side + near], weight).astype(jnp.bfloat16)
     own = dot_last(act[:side], weight)
-    far_sum = paired(far_sum, "tensor", 1)
-    near_sum = paired(near_sum, "tensor", 1)
+    far_sum = paired(far_sum, TENSOR, 1)
+    near_sum = paired(near_sum, TENSOR, 1)
     spots = {key: i * rows for i, key in enumerate(received_order(count))}
 
     def part(hops, lag):
@@ -472,9 +473,9 @@
         lead = hop(lead, hops, False)
         if hops < half:
             lag = hop(lag, hops, True)
-        if hops == half - 1:
+        if hops == half:
             token = lead
-    across = paired(lag, "tensor", 1)
+    across = paired(lag, TENSOR, 1)
     return part(0, False) + lead.astype(jnp.float32) + across.astype(jnp.float32), token
 
 
@@ -501,6 +502,32 @@
         out_specs=whole_vmem(len(widths)),
         cost_estimate=pl.CostEstimate(flops=0, bytes_accessed=2 * size, transcendentals=0),
     )(flags, *blocks)
+
+
+def packed(pairs, flags, count):
+    rows = pairs[0][0].shape[0] // count
+    widths = [kept.shape[1] for kept, _ in pairs]
+
+    def kernel(flags_ref, *refs):
+        ins, outs = refs[: 2 * len(pairs)], refs[2 * len(pairs) :]
+        for s, out in enumerate(outs):
+            at = pl.ds(pl.multiple_of((flags_ref[0] ^ s) * rows, rows), rows)
+            left = 0
+            for i, width in enumerate(widths):
+                value = ins[2 * i][at, :].astype(jnp.float32)
+                value += ins[2 * i + 1][at, :].astype(jnp.float32)
+                out[:, left : left + width] = value.astype(out.dtype)
+                left += width
+
+    operands = [array for pair in pairs for array in pair]
+    size = 2 * count * rows * sum(widths)
+    return pl.pallas_call(
+        kernel,
+        out_shape=[jax.ShapeDtypeStruct((rows, sum(widths)), jnp.bfloat16)] * count,
+        in_specs=[pl.BlockSpec(memory_space=pltpu.SMEM)] + whole_vmem(len(operands)),
+        out_specs=whole_vmem(count),
+        cost_estimate=pl.CostEstimate(flops=0, bytes_accessed=3 * size, transcendentals=0),
+    )(flags, *operands)
 
 
 def place_columns(first, second, flags, widths, shared, skip):
@@ -588,10 +615,10 @@
     query_gain,
     key_gain,
 ):
-    count = lax.axis_size("dp")
-    plane = lax.axis_index("section")
-    me = lax.axis_index("dp")
-    core = lax.axis_index("tensor")
+    count = lax.axis_size(DP)
+    plane = lax.axis_index(SECTION)
+    me = lax.axis_index(DP)
+    core = lax.axis_index(TENSOR)
     flags = jnp.stack([me, plane]).astype(jnp.int32)
     model_width = inputs.shape[2]
     rows = inputs.shape[1] // 2
@@ -601,7 +628,7 @@
     gain_width = attn_gain.shape[1]
 
     def by_layer(own):
-        theirs = paired(own, "section", 1)
+        theirs = paired(own, SECTION, 1)
         first = plane == 0
         return [jnp.where(first, own, theirs), jnp.where(first, theirs, own)]
 
@@ -623,7 +650,7 @@
     gains = jnp.concatenate(by_layer(gains.astype(jnp.float32)))
     docs = lax.dynamic_index_in_dim(segments, plane, 0, keepdims=False).astype(jnp.float32)
     note = jnp.concatenate([gains, docs])
-    notes = jnp.stack([note] + [paired(note, "dp", s) for s in range(1, count)])
+    notes = jnp.stack([note] + [paired(note, DP, s) for s in range(1, count)])
     notes = jnp.concatenate(
         [lax.dynamic_slice_in_dim(notes, me ^ j, 1, axis=0) for j in range(count)], axis=0
     )
@@ -663,8 +690,10 @@
         def block(to):
             return jnp.concatenate(
                 [
-                    lax.dynamic_slice_in_dim(array, (to // share) * width, width, axis=1)
-                    for array, width, share in pieces
+                    lax.dynamic_slice_in_dim(
+                        array, (to // share) * stride + skip, width, axis=1
+                    )
+                    for array, width, share, stride, skip in pieces
                 ],
                 axis=1,
             )
@@ -672,23 +701,34 @@
         return [block(me ^ s) for s in range(count)]
 
     def turn(blocks):
-        return [blocks[0]] + [paired(blocks[s], "dp", s) for s in range(1, count)]
+        moved = [blocks[0]]
+        for s in range(1, count):
+            moved.append(paired(blocks[s], DP, s))
+        return moved
 
     def both_layers(blocks, widths):
         sets = []
         for placed in place_rows(blocks, flags, widths):
-            facing = paired(placed, "section", 1)
+            facing = paired(placed, SECTION, 1)
             sets.append([jnp.where(plane == layer, placed, facing) for layer in range(2)])
         return sets
 
-    pieces_of = {
-        "qk": ((w_query[0], head_size, 1), (key_weight[0], head_size, group_size)),
-        "vo": ((value_weight[0], head_size, group_size), (w_output[0], head_size, 1)),
-        "g": ((w_gate[0], ff_width, 1),),
-        "u": ((w_up[0], ff_width, 1),),
-        "d": ((w_down[0], ff_width, 1),),
+    wide = ff_width * 2 // 3
+
+    def heads(array, share):
+        return (array[0], head_size, share, head_size, 0)
+
+    def hidden(array, width, skip):
+        return (array[0], width, 1, ff_width, skip)
+
+    sliced = {
+        "qk": cut((heads(w_query, 1), heads(key_weight, group_size))),
+        "vo": cut((heads(value_weight, group_size), heads(w_output, 1))),
+        "g": cut((hidden(w_gate, ff_width, 0),)),
+        "u": cut((hidden(w_up, ff_width, 0),)),
+        "d": cut((hidden(w_down, wide, 0),)),
+        "e": cut((hidden(w_down, ff_width - wide, wide),)),
     }
-    sliced = {name: cut(pieces) for name, pieces in pieces_of.items()}
     turned, weights = {}, {}
 
     def attention(raw, value, layer):
@@ -732,12 +772,17 @@
         if layer == 0:
             weights["u"] = both_layers(gate(turned["u"], token), (ff_width,))[0]
             turned["d"] = turn(gate(sliced["d"], turned["u"]))
+            turned["e"] = turn(gate(sliced["e"], turned["d"]))
             weights["gu"] = [
                 jnp.concatenate([weights["g"][i], weights["u"][i]], axis=1) for i in range(2)
             ]
         parts, token = gather_ring(rms_scale(mixed, gain_mlp).astype(jnp.bfloat16))
         if layer == 0:
-            weights["d"] = both_layers(gate(turned["d"], parts[1]), (ff_width,))[0]
+            weights["d"] = both_layers(gate(turned["d"], token), (wide,))[0]
+            weights["e"] = both_layers(gate(turned["e"], parts[1]), (ff_width - wide,))[0]
+            weights["d"] = [
+                jnp.concatenate([weights["d"][i], weights["e"][i]], axis=1) for i in range(2)
+            ]
         normed_mlp, raw_mlp = multiplied(parts, weights["gu"][layer])
         gate_raw, up_raw = raw_mlp[:, :ff_width], raw_mlp[:, ff_width:]
         activated = swiglu(gate_raw, up_raw).astype(jnp.bfloat16)
@@ -753,26 +798,25 @@
     def halves(grad):
         span = grad.shape[0] // 2
         sent = lax.dynamic_slice_in_dim(grad, (1 - plane) * span, span, axis=0)
-        kept = lax.dynamic_slice_in_dim(grad, plane * span, span, axis=0)
-        return kept, paired(sent.astype(jnp.bfloat16), "section", 1)
-
-    last_turn = []
-
-    def returned(pair, token):
-        kept, taken = pair
+        kept = lax.dynamic_slice_in_dim(grad, plane * span, span, axis=0).astype(jnp.bfloat16)
+        return kept, paired(sent.astype(jnp.bfloat16), SECTION, 1)
+
+    turns = []
+
+    def returned(pairs, token):
         if token is not None:
-            taken = gate(taken, token)
-        total = (kept + taken.astype(jnp.float32)).astype(jnp.bfloat16)
-        blocks = [lax.dynamic_slice_in_dim(total, (me ^ s) * part, part, axis=0) for s in range(count)]
-        if last_turn:
-            blocks = gate(blocks, last_turn[-1])
-        last_turn.append(turn(blocks))
-        return last_turn[-1]
+            pairs = [(kept, gate(taken, token)) for kept, taken in pairs]
+        if len(turns) > 1:
+            pairs = [(kept, gate(taken, turns[-2])) for kept, taken in pairs]
+        turns.append(turn(packed(pairs, flags, count)))
+        return turns[-1]
 
     def backward(gathered, grad_out, stored, layer, back, late):
         layer_in, normed, kept, attn, mixed, normed_mlp, gate_raw, up_raw, activated = stored
         queries, key_raw, value, query_rot, key_rot, log_total = kept
         gain_attn, gain_mlp, gain_q, gain_k = layer_gains[layer]
+        if late is not None:
+            late = late(None)
         out_low, act_grad = multiplied(gathered, weights["d"][layer])
         unused, swiglu_back = jax.vjp(swiglu, gate_raw, up_raw)
         gate_grad, up_grad = swiglu_back(act_grad)
@@ -784,12 +828,9 @@
         unused, mlp_norm_back = jax.vjp(rms_scale, mixed, gain_mlp)
         mixed_part, grad_gain_mlp = mlp_norm_back(summed)
         mixed_grad = grad_out + mixed_part
-        back["d"] = returned(sums["d"], mixed_grad)
         parts, token = gather_ring(mixed_grad.astype(jnp.bfloat16))
-        branch_low, attn_grad = multiplied(parts, weights["o"][layer])
-        if late is not None:
-            late = partial(late, attn_grad)
-        back["gu"] = returned(sums["gu"], parts[1])
+        attn_grad = by_parts(parts, weights["o"][layer])
+        back["mlp"] = returned((sums["gu"], sums["d"]), parts[1])
         query_back, key_back, value_back = head_attend_back(
             query_rot, key_rot, value, allowed, log_total, attn_grad.astype(jnp.bfloat16)
         )
@@ -798,22 +839,18 @@
         unused, query_rope_back = jax.vjp(rope, queries, gain_q)
         query_grad, grad_gain_q = query_rope_back(query_back)
         qkv_grad = jnp.concatenate([query_grad, key_grad, value_back], axis=1).astype(jnp.bfloat16)
-        if late is not None:
-            late = late()
-            qkv_grad = gate(qkv_grad, late[0])
         summed, token = product_scattered(qkv_grad, weights["qkv"][layer])
-        two = 2 * head_size
-        grad_vo = [dot_first(normed, qkv_grad[:, two:]), dot_first(branch_low, attn)]
-        grad_vo = jnp.concatenate(grad_vo, axis=1)
-        grad_qk = dot_first(normed, qkv_grad[:, :two])
-        if layer == 0:
-            sums = (halves(grad_qk), halves(grad_vo))
-        else:
-            sums = halves(jnp.concatenate([grad_qk, grad_vo], axis=1))
+        grad_o, top = 0.0, 0
+        for rows_part in parts:
+            span = rows_part.shape[0]
+            grad_o = grad_o + dot_first(rows_part, attn[top : top + span])
+            top += span
+        grad_attn = jnp.concatenate([dot_first(normed, qkv_grad), grad_o], axis=1)
+        sums = halves(grad_attn)
         unused, attn_norm_back = jax.vjp(rms_scale, layer_in, gain_attn)
         input_part, grad_gain_attn = attn_norm_back(summed)
         small = (grad_gain_attn, grad_gain_mlp, grad_gain_q, grad_gain_k)
-        points = (branch_low, token)
+        points = token
         return mixed_grad + input_part, sums, small, points, late
 
     finish, stored_first, _ = forward(own_rows(inputs).astype(jnp.float32), 0)
@@ -829,34 +866,35 @@
     out_second = last[0]
     grad_second = grad_second.astype(jnp.bfloat16)
     gathered, _ = gather_ring(grad_second)
-    back_second["attn"] = returned(waiting, gathered[1])
+    back_second["attn"] = returned((waiting,), gathered[1])
     grad_first, waiting, small_first, points, last = backward(
         gathered, grad_second.astype(jnp.float32), stored_first, 0, back_first, None
     )
     grad_first = grad_first.astype(jnp.bfloat16)
-    back_first["qk"] = returned(waiting[0], None)
-    back_first["vo"] = returned(waiting[1], None)
+    back_first["attn"] = returned((waiting,), None)
 
     def by_section(first, second):
         first, second = unhalved(first), unhalved(second)
         kept = jnp.where(plane == 0, first, second)
-        taken = paired(jnp.where(plane == 0, second, first), "section", 1)
+        taken = paired(jnp.where(plane == 0, second, first), SECTION, 1)
         both = jnp.where(plane == 0, jnp.stack([kept, taken]), jnp.stack([taken, kept]))
-        facing = paired(both, "tensor", 1)
-        return jnp.where(
+        facing = paired(both, TENSOR, 1)
+        whole = jnp.where(
             core == 0,
             jnp.concatenate([both, facing], axis=1),
             jnp.concatenate([facing, both], axis=1),
-        )[None]
-
-    section_out = by_section(out_first, out_second)
-    input_grads = by_section(grad_first, grad_second)
+        )
+        return whole[None], facing
+
+    section_out, _ = by_section(out_first, out_second)
+    input_grads, facing = by_section(grad_first, grad_second)
 
     def owned(name, widths, shared, token, other=None, skip=0):
-        firsts = back_first[name] if token is None else gate(back_first[name], token)
-        seconds = back_second[other or name]
+        firsts, seconds = back_first[name], back_second[other or name]
         kept, sent = place_columns(firsts, seconds, flags, widths, shared, skip)
-        taken = paired(sent, "section", 1)
+        taken = paired(sent, SECTION, 1)
+        if token is not None:
+            taken = gate(taken, token)
         both = jnp.where(
             plane == 0,
             jnp.concatenate([kept, taken], axis=0),
@@ -864,17 +902,14 @@
         )
         return both.astype(jnp.float32)
 
-    branch_point, summed_point = points
     ff_total = w_gate.shape[2]
-    grad_d = owned("d", (ff_width,), (False,), branch_point)
-    grad_gu = owned("gu", (ff_width,) * 2, (False,) * 2, summed_point)
-    grad_qk = owned("qk", (head_size,) * 2, (False, True), None, "attn")
-    grad_vo = owned("vo", (head_size,) * 2, (True, False), None, "attn", 2 * head_size)
-    q_total, v_total = w_query.shape[2], value_weight.shape[2]
-    attn_grads = (
-        grad_qk[:, :q_total], grad_qk[:, q_total:], grad_vo[:, :v_total], grad_vo[:, v_total:],
-    )
-    mlp_grads = (grad_gu[:, :ff_total], grad_gu[:, ff_total:], grad_d)
+    grad_mlp = owned("mlp", (ff_width,) * 3, (False,) * 3, None)
+    grad_attn = owned("attn", (head_size,) * 4, (False, True, True, False), facing)
+    edges = [0]
+    for array in (w_query, key_weight, value_weight, w_output):
+        edges.append(edges[-1] + array.shape[2])
+    attn_grads = [grad_attn[:, a:b] for a, b in zip(edges, edges[1:])]
+    mlp_grads = [grad_mlp[:, i * ff_total : (i + 1) * ff_total] for i in range(3)]
 
     rows_of = jnp.concatenate(
         [
@@ -896,11 +931,11 @@
         gain_sum = gain_sum.reshape(2, step, -1)
         kept = lax.dynamic_index_in_dim(gain_sum, bit, 0, keepdims=False)
         sent = lax.dynamic_index_in_dim(gain_sum, 1 - bit, 0, keepdims=False)
-        gain_sum = kept + paired(sent, "dp", step)
+        gain_sum = kept + paired(sent, DP, step)
         step //= 2
     gain_sum = gain_sum.reshape(-1)
-    gain_sum = gain_sum + paired(gain_sum, "tensor", 1)
-    gain_sum = gain_sum + paired(gain_sum, "section", 1)
+    gain_sum = gain_sum + paired(gain_sum, TENSOR, 1)
+    gain_sum = gain_sum + paired(gain_sum, SECTION, 1)
     mine = jnp.where(plane == 0, gain_sum[:per_layer], gain_sum[per_layer:])
     grad_gain_attn = mine[:gain_width]
     grad_gain_mlp = mine[gain_width : 2 * gain_width]
@@ -916,7 +951,7 @@
 
 def fits(mesh):
     sizes = dict(mesh.shape)
-    return sizes["dp"] == 8 and sizes["tensor"] == 2 and sizes["section"] == 2
+    return sizes[DP] == 8 and sizes[TENSOR] == 2 and sizes[SECTION] == 2
 
 
 def solution(mesh):
@@ -924,35 +959,35 @@
         per_device if fits(mesh) else per_device_wide,
         mesh=mesh,
         in_specs=(
-            P(None, "dp", None),
-            P(None, "dp", None),
-            P(None, "dp"),
-            P("section", "dp", "tensor"),
-            P("section", "dp", "tensor"),
-            P("section", "dp", "tensor"),
-            P("section", "dp", "tensor"),
-            P("section", "dp", "tensor"),
-            P("section", "dp", "tensor"),
-            P("section", "dp", "tensor"),
-            P("section", "dp"),
-            P("section", "dp"),
-            P("section", None),
-            P("section", None),
+            P(None, DP, None),
+            P(None, DP, None),
+            P(None, DP),
+            P(SECTION, DP, TENSOR),
+            P(SECTION, DP, TENSOR),
+            P(SECTION, DP, TENSOR),
+            P(SECTION, DP, TENSOR),
+            P(SECTION, DP, TENSOR),
+            P(SECTION, DP, TENSOR),
+            P(SECTION, DP, TENSOR),
+            P(SECTION, DP),
+            P(SECTION, DP),
+            P(SECTION, None),
+            P(SECTION, None),
         ),
         out_specs=(
-            P("section", None, "dp", None),
-            P("section", None, "dp", None),
-            P("section", "dp", "tensor"),
-            P("section", "dp", "tensor"),
-            P("section", "dp", "tensor"),
-            P("section", "dp", "tensor"),
-            P("section", "dp", "tensor"),
-            P("section", "dp", "tensor"),
-            P("section", "dp", "tensor"),
-            P("section", "dp"),
-            P("section", "dp"),
-            P("section", None),
-            P("section", None),
+            P(SECTION, None, DP, None),
+            P(SECTION, None, DP, None),
+            P(SECTION, DP, TENSOR),
+            P(SECTION, DP, TENSOR),
+            P(SECTION, DP, TENSOR),
+            P(SECTION, DP, TENSOR),
+            P(SECTION, DP, TENSOR),
+            P(SECTION, DP, TENSOR),
+            P(SECTION, DP, TENSOR),
+            P(SECTION, DP),
+            P(SECTION, DP),
+            P(SECTION, None),
+            P(SECTION, None),
         ),
         check_vma=False,
     )

time: 1210 us -> 1180 us (0.975)
  starting transfers between devices: 357 us -> 324 us
  waiting for transfers between devices: 484 us -> 452 us
    ppermute x112, starting transfers between devices: 164 us -> 119 us  [ring(): return lax.ppermute(x, (TENSOR, DP), pairs)]
    ppermute x166 -> x150, waiting for transfers between devices: 248 us -> 226 us  [paired(): return lax.ppermute(x, axis, [(i, i ^ flip) for i in range(count)])]
    pallas_call x0 -> x4, Pallas kernels: none -> 13.8 us  [packed(): pl.pallas_call(kernel, out_shape=[jax.ShapeDtypeStruct((rows, sum(widths)...]
    ppermute x166 -> x150, starting transfers between devices: 192 us -> 205 us  [paired(): return lax.ppermute(x, axis, [(i, i ^ flip) for i in range(count)])]
    unnamed x655 -> x669, local copies, waits for them, and re-layouts: 21.2 us -> 27.1 us
    dot_general x14 -> x18, matrix products: 34.3 us -> 39.5 us  [dot_first(): lax.dot_general(left, right, (((0,), (0,)), ((), ())), preferred_element_...]
  transfers between devices with their start and end apart: 278 -> 262, of which waited for: 119 -> 113; matrix products, arithmetic and copies ran while one was open for 18% -> 20% of each run, Pallas kernels for 5% -> 6%
where the time goes in v3:
time: 1180 us; the launch traced here: 1170 us
  waiting for transfers between devices  452 us (38%)
  starting transfers between devices  324 us (27%)
  matrix products  128 us (11%)
  other arithmetic  116 us (10%)
  Pallas kernels  81.7 us (7%)
  local copies, waits for them, and re-layouts  65.4 us (6%)
    ppermute x112, waiting for transfers between devices, ring(): return lax.ppermute(x, (TENSOR, DP), pairs)  227 us
    ppermute x150, waiting for transfers between devices, paired(): return lax.ppermute(x, axis, [(i, i ^ flip) for i in range(count)])  226 us
    ppermute x150, starting transfers between devices, paired(): return lax.ppermute(x, axis, [(i, i ^ flip) for i in range(count)])  205 us
    ppermute x112, starting transfers between devices, ring(): return lax.ppermute(x, (TENSOR, DP), pairs)  119 us
    dot_general x37, matrix products, dot_plain(): return jnp.dot(left, right, preferred_element_type=jnp.float32)  55.4 us
    pallas_call x17, Pallas kernels, joined(): pl.pallas_call(kernel, out_shape=jax.ShapeDtypeStruct((rows, width), piec...  40.8 us
    dot_general x18, matrix products, dot_first(): lax.dot_general(left, right, (((0,), (0,)), ((), ())), preferred_element_...  39.5 us
    dot_general x28, matrix products, dot_last(): lax.dot_general(left, right, (((1,), (1,)), ((), ())), preferred_element_...  33.4 us
  transfers between devices with their start and end apart: 262, of which 113 were waited for; matrix products, arithmetic and copies ran while one was open for 20% of the time, Pallas kernels for 6%

profile of v3, /device:TPU:0, one launch (start us, length us, event | category | flops | bytes accessed | tf_op | source)
XLA Modules:
  0.0 1173.5 jit_solution(5145446679689794733)
XLA Ops:
  61.4 6.6 collective-permute-start.30
  108.5 16.6 %collective-permute-done.34 = bf16[2048,128]{1,0:T(8,128)(2,1)} collective-permute-done((bf16[2048,128]{1,0:T(8,128)(2,1)S(1)}, bf16[2048,128]{1,0:T(8,128)(2,1)}, u32[]{:S(2)}, u32[]{:S(2)}) %collective-permute-start.34) | collective-permute-done | bytes 524320 | tf_op jit(solution)/shard_map/ppermute | solution.py:368
  158.2 7.5 collective-permute-done.37
  193.4 7.9 collective-permute-done.52.refs_2_
  209.7 8.8 collective-permute-done.55.refs_5_
  219.4 7.5 collective-permute-start.60
  245.7 12.0 %collective-permute-done.63.refs_5_ = bf16[256,384]{1,0:T(8,128)(2,1)S(1)} collective-permute-done((bf16[256,384]{1,0:T(8,128)(2,1)S(1)}, bf16[256,384]{1,0:T(8,128)(2,1)S(1)}, u32[]{:S(2)}, u32[]{:S(2)}) %collective-permute-start.63) | collective-permute-done | bytes 196640 | tf_op jit(solution)/shard_map/ppermute | solution.py:368
  260.9 7.1 collective-permute-start.72
  279.6 7.1 collective-permute-done.73.refs_3_
  296.0 10.6 collective-permute-done.75.refs_5_
  307.8 7.0 collective-permute-done.76.refs_6_
  364.5 24.4 %collective-permute-done.86 = bf16[2048,128]{1,0:T(8,128)(2,1)S(1)} collective-permute-done((bf16[2048,128]{1,0:T(8,128)(2,1)}, bf16[2048,128]{1,0:T(8,128)(2,1)S(1)}, u32[]{:S(2)}, u32[]{:S(2)}) %collective-permute-start.86) | collective-permute-done | bytes 524320 | tf_op jit(solution)/shard_map/ppermute | solution.py:368
  854.9 10.5 collective-permute-done.222.refs_1_
  870.4 7.4 fusion.12
  925.9 22.3 %collective-permute-done.244.refs_12_ = bf16[128,1152]{1,0:T(8,128)(2,1)S(1)} collective-permute-done((bf16[128,1152]{1,0:T(8,128)(2,1)S(1)}, bf16[128,1152]{1,0:T(8,128)(2,1)S(1)}, u32[]{:S(2)}, u32[]{:S(2)}) %collective-permute-start.244) | collective-permute-done | bytes 294944 | tf_op jit(solution)/shard_map/ppermute | solution.py:368
  951.7 9.1 collective-permute-done.245.refs_13_
  962.9 11.1 collective-permute-start.224
  1021.7 6.4 collective-permute-done.250.refs_2_
  1040.6 18.5 %collective-permute-done.253.refs_5_ = bf16[128,1152]{1,0:T(8,128)(2,1)S(1)} collective-permute-done((bf16[128,1152]{1,0:T(8,128)(2,1)}, bf16[128,1152]{1,0:T(8,128)(2,1)S(1)}, u32[]{:S(2)}, u32[]{:S(2)}) %collective-permute-start.253) | collective-permute-done | bytes 294944 | tf_op jit(solution)/shard_map/ppermute | solution.py:368
  1073.8 15.3 %collective-permute-start.230 = (bf16[128,512]{1,0:T(8,128)(2,1)}, bf16[128,512]{1,0:T(8,128)(2,1)}, u32[]{:S(2)}, u32[]{:S(2)}) collective-permute-start(bf16[128,512]{1,0:T(8,128)(2,1)} %get-tuple-element.301), channel_id=1, source_target_pairs={{0,1},{1,0},{2,3},{3,2},{4,5},{5,4},{6,7},{7,6},{8,9},{9,8},{10,11... | collective-permute-start | bytes 393224 | tf_op jit(solution)/shard_map/ppermute | solution.py:368
  1098.9 7.1 collective-permute-done.233.refs_4_
  1133.0 8.9 fusion.3
  1142.0 7.0 collective-permute-start.258
  1157.1 7.8 slice_bitcast_fusion
  (1511 shorter events, 912.8 us)
Async XLA Ops:
  231.6 42.4 %collective-permute-start.40 = (bf16[64,2048]{1,0:T(8,128)(2,1)S(1)}, bf16[64,2048]{1,0:T(8,128)(2,1)S(1)}, u32[]{:S(2)}, u32[]{:S(2)}) collective-permute-start(bf16[64,2048]{1,0:T(8,128)(2,1)S(1)} %get-tuple-element.394), channel_id=1, source_target_pairs={{0,1},{2,0},{4,2},{6,4},{7,6},{5,7},{3,5},{1,3},{8,10},{10,12},{12... | collective-permute-start | bytes 786440 | tf_op jit(solution)/shard_map/ppermute | solution.py:382
  233.7 42.0 %collective-permute-start.44 = (bf16[64,2048]{1,0:T(8,128)(2,1)}, bf16[64,2048]{1,0:T(8,128)(2,1)}, u32[]{:S(2)}, u32[]{:S(2)}) collective-permute-start(bf16[64,2048]{1,0:T(8,128)(2,1)} %collective-permute-done.43), channel_id=1, source_target_pairs={{0,8},{8,0},{1,9},{9,1},{2,10},{10,2},{3,11},{11,3},{4,12},{12,4},... | collective-permute-start | bytes 786440 | tf_op jit(solution)/shard_map/ppermute | solution.py:368
  270.8 52.9 %collective-permute-start.58 = (bf16[2048,384]{1,0:T(8,128)(2,1)}, bf16[2048,384]{1,0:T(8,128)(2,1)}, u32[]{:S(2)}, u32[]{:S(2)}) collective-permute-start(bf16[2048,384]{1,0:T(8,128)(2,1)} %shard_map.243), channel_id=1, source_target_pairs={{0,16},{16,0},{1,17},{17,1},{2,18},{18,2},{3,19},{19,3},{4,20},{20... | collective-permute-start | bytes 4718600 | tf_op jit(solution)/shard_map/ppermute | solution.py:368
  274.1 65.7 %collective-permute-start.66 = (bf16[2048,384]{1,0:T(8,128)(2,1)}, bf16[2048,384]{1,0:T(8,128)(2,1)}, u32[]{:S(2)}, u32[]{:S(2)}) collective-permute-start(bf16[2048,384]{1,0:T(8,128)(2,1)} %shard_map.244), channel_id=1, source_target_pairs={{0,16},{16,0},{1,17},{17,1},{2,18},{18,2},{3,19},{19,3},{4,20},{20... | collective-permute-start | bytes 4718600 | tf_op jit(solution)/shard_map/ppermute | solution.py:368
  354.5 36.1 %collective-permute-start.78 = (bf16[2048,256]{1,0:T(8,128)(2,1)}, bf16[2048,256]{1,0:T(8,128)(2,1)}, u32[]{:S(2)}, u32[]{:S(2)}) collective-permute-start(bf16[2048,256]{1,0:T(8,128)(2,1)} %shard_map.246), channel_id=1, source_target_pairs={{0,16},{16,0},{1,17},{17,1},{2,18},{18,2},{3,19},{19,3},{4,20},{20... | collective-permute-start | bytes 3145736 | tf_op jit(solution)/shard_map/ppermute | solution.py:368
  355.0 38.7 %collective-permute-start.69 = (bf16[320,2048]{1,0:T(8,128)(2,1)}, bf16[320,2048]{1,0:T(8,128)(2,1)}, u32[]{:S(2)}, u32[]{:S(2)}) collective-permute-start(bf16[320,2048]{1,0:T(8,128)(2,1)} %shard_map.242), channel_id=1, source_target_pairs={{0,8},{8,0},{1,9},{9,1},{2,10},{10,2},{3,11},{11,3},{4,12},{12,4},... | collective-permute-start | bytes 3932168 | tf_op jit(solution)/shard_map/ppermute | solution.py:368
  721.0 58.9 %collective-permute-start.135 = (bf16[320,2048]{1,0:T(8,128)(2,1)}, bf16[320,2048]{1,0:T(8,128)(2,1)}, u32[]{:S(2)}, u32[]{:S(2)}) collective-permute-start(bf16[320,2048]{1,0:T(8,128)(2,1)} %convolution_convert_fusion.6), channel_id=1, source_target_pairs={{0,8},{8,0},{1,9},{9,1},{2,10},{10,2},{3,11},{11,3},{4,12},{12,4},... | collective-permute-start | bytes 3932168 | tf_op jit(solution)/shard_map/ppermute | solution.py:368
  775.7 73.1 %collective-permute-start.240 = (bf16[1024,384]{1,0:T(8,128)(2,1)}, bf16[1024,384]{1,0:T(8,128)(2,1)}, u32[]{:S(2)}, u32[]{:S(2)}) collective-permute-start(bf16[1024,384]{1,0:T(8,128)(2,1)} %get-tuple-element.439), channel_id=1, source_target_pairs={{0,16},{16,0},{1,17},{17,1},{2,18},{18,2},{3,19},{19,3},{4,20},{20... | collective-permute-start | bytes 2359304 | tf_op jit(solution)/shard_map/ppermute | solution.py:368
  776.3 72.5 %collective-permute-start.239 = (bf16[1024,768]{1,0:T(8,128)(2,1)}, bf16[1024,768]{1,0:T(8,128)(2,1)}, u32[]{:S(2)}, u32[]{:S(2)}) collective-permute-start(bf16[1024,768]{1,0:T(8,128)(2,1)} %get-tuple-element.416), channel_id=1, source_target_pairs={{0,16},{16,0},{1,17},{17,1},{2,18},{18,2},{3,19},{19,3},{4,20},{20... | collective-permute-start | bytes 4718600 | tf_op jit(solution)/shard_map/ppermute | solution.py:368
  801.7 37.1 %collective-permute-start.143 = (bf16[64,2048]{1,0:T(8,128)(2,1)S(1)}, bf16[64,2048]{1,0:T(8,128)(2,1)S(1)}, u32[]{:S(2)}, u32[]{:S(2)}) collective-permute-start(bf16[64,2048]{1,0:T(8,128)(2,1)S(1)} %fusion.165), channel_id=1, source_target_pairs={{0,1},{2,0},{4,2},{6,4},{7,6},{5,7},{3,5},{1,3},{8,10},{10,12},{12... | collective-permute-start | bytes 786440 | tf_op jit(solution)/shard_map/ppermute | solution.py:382
  853.0 65.5 %collective-permute-start.241 = (bf16[128,1152]{1,0:T(8,128)(2,1)}, bf16[128,1152]{1,0:T(8,128)(2,1)}, u32[]{:S(2)}, u32[]{:S(2)}) collective-permute-start(bf16[128,1152]{1,0:T(8,128)(2,1)} %get-tuple-element.315), channel_id=1, source_target_pairs={{0,1},{1,0},{2,3},{3,2},{4,5},{5,4},{6,7},{7,6},{8,9},{9,8},{10,11... | collective-permute-start | bytes 884744 | tf_op jit(solution)/shard_map/ppermute | solution.py:368
  854.5 67.6 %collective-permute-start.242 = (bf16[128,1152]{1,0:T(8,128)(2,1)}, bf16[128,1152]{1,0:T(8,128)(2,1)}, u32[]{:S(2)}, u32[]{:S(2)}) collective-permute-start(bf16[128,1152]{1,0:T(8,128)(2,1)} %get-tuple-element.316), channel_id=1, source_target_pairs={{0,2},{1,3},{2,0},{3,1},{4,6},{5,7},{6,4},{7,5},{8,10},{9,11},{10,... | collective-permute-start | bytes 884744 | tf_op jit(solution)/shard_map/ppermute | solution.py:368
  904.3 45.8 %collective-permute-start.248 = (bf16[1024,384]{1,0:T(8,128)(2,1)S(1)}, bf16[1024,384]{1,0:T(8,128)(2,1)S(1)}, u32[]{:S(2)}, u32[]{:S(2)}) collective-permute-start(bf16[1024,384]{1,0:T(8,128)(2,1)S(1)} %copy-done.141), channel_id=1, source_target_pairs={{0,16},{16,0},{1,17},{17,1},{2,18},{18,2},{3,19},{19,3},{4,20},{20... | collective-permute-start | bytes 2359304 | tf_op jit(solution)/shard_map/ppermute | solution.py:368
  905.3 68.7 %collective-permute-start.238 = (bf16[1024,768]{1,0:T(8,128)(2,1)S(1)}, bf16[1024,768]{1,0:T(8,128)(2,1)}, u32[]{:S(2)}, u32[]{:S(2)}) collective-permute-start(bf16[1024,768]{1,0:T(8,128)(2,1)S(1)} %copy-done.84), channel_id=1, source_target_pairs={{0,16},{16,0},{1,17},{17,1},{2,18},{18,2},{3,19},{19,3},{4,20},{20... | collective-permute-start | bytes 4718600 | tf_op jit(solution)/shard_map/ppermute | solution.py:368
  922.1 38.7 %collective-permute-start.245 = (bf16[128,1152]{1,0:T(8,128)(2,1)S(1)}, bf16[128,1152]{1,0:T(8,128)(2,1)S(1)}, u32[]{:S(2)}, u32[]{:S(2)}) collective-permute-start(bf16[128,1152]{1,0:T(8,128)(2,1)S(1)} %copy-done.322), channel_id=1, source_target_pairs={{0,5},{1,4},{2,7},{3,6},{4,1},{5,0},{6,3},{7,2},{8,13},{9,12},{10,... | collective-permute-start | bytes 884744 | tf_op jit(solution)/shard_map/ppermute | solution.py:368
  925.0 36.4 %collective-permute-start.246 = (bf16[128,1152]{1,0:T(8,128)(2,1)S(1)}, bf16[128,1152]{1,0:T(8,128)(2,1)S(1)}, u32[]{:S(2)}, u32[]{:S(2)}) collective-permute-start(bf16[128,1152]{1,0:T(8,128)(2,1)S(1)} %copy-done.321), channel_id=1, source_target_pairs={{0,6},{1,7},{2,4},{3,5},{4,2},{5,3},{6,0},{7,1},{8,14},{9,15},{10,... | collective-permute-start | bytes 884744 | tf_op jit(solution)/shard_map/ppermute | solution.py:368
  960.8 38.2 %collective-permute-start.145 = (bf16[64,2048]{1,0:T(8,128)(2,1)}, bf16[64,2048]{1,0:T(8,128)(2,1)S(1)}, u32[]{:S(2)}, u32[]{:S(2)}) collective-permute-start(bf16[64,2048]{1,0:T(8,128)(2,1)} %select_n.839), channel_id=1, source_target_pairs={{0,16},{16,0},{1,17},{17,1},{2,18},{18,2},{3,19},{19,3},{4,20},{20... | collective-permute-start | bytes 786440 | tf_op jit(solution)/shard_map/ppermute | solution.py:368
  961.3 39.3 %collective-permute-start.223 = (bf16[128,512]{1,0:T(8,128)(2,1)}, bf16[128,512]{1,0:T(8,128)(2,1)S(1)}, u32[]{:S(2)}, u32[]{:S(2)}) collective-permute-start(bf16[128,512]{1,0:T(8,128)(2,1)} %get-tuple-element.292), channel_id=1, source_target_pairs={{0,1},{1,0},{2,3},{3,2},{4,5},{5,4},{6,7},{7,6},{8,9},{9,8},{10,11... | collective-permute-start | bytes 393224 | tf_op jit(solution)/shard_map/ppermute | solution.py:368
  962.9 39.0 %collective-permute-start.224 = (bf16[128,512]{1,0:T(8,128)(2,1)}, bf16[128,512]{1,0:T(8,128)(2,1)}, u32[]{:S(2)}, u32[]{:S(2)}) collective-permute-start(bf16[128,512]{1,0:T(8,128)(2,1)} %get-tuple-element.293), channel_id=1, source_target_pairs={{0,2},{1,3},{2,0},{3,1},{4,6},{5,7},{6,4},{7,5},{8,10},{9,11},{10,... | collective-permute-start | bytes 393224 | tf_op jit(solution)/shard_map/ppermute | solution.py:368
  1016.7 54.4 %collective-permute-start.221 = (bf16[1024,512]{1,0:T(8,128)(2,1)}, bf16[1024,512]{1,0:T(8,128)(2,1)}, u32[]{:S(2)}, u32[]{:S(2)}) collective-permute-start(bf16[1024,512]{1,0:T(8,128)(2,1)} %get-tuple-element.431), channel_id=1, source_target_pairs={{0,16},{16,0},{1,17},{17,1},{2,18},{18,2},{3,19},{19,3},{4,20},{20... | collective-permute-start | bytes 3145736 | tf_op jit(solution)/shard_map/ppermute | solution.py:368
  1028.1 61.1 %collective-permute-start.146 = (bf16[2,64,2048]{2,1,0:T(8,128)(2,1)}, bf16[2,64,2048]{2,1,0:T(8,128)(2,1)}, u32[]{:S(2)}, u32[]{:S(2)}) collective-permute-start(bf16[2,64,2048]{2,1,0:T(8,128)(2,1)} %maximum_select_fusion.4), channel_id=1, source_target_pairs={{0,8},{8,0},{1,9},{9,1},{2,10},{10,2},{3,11},{11,3},{4,12},{12,4},... | collective-permute-start | bytes 1572872 | tf_op jit(solution)/shard_map/ppermute | solution.py:368
  1064.1 34.6 %collective-permute-start.217 = (bf16[64,2048]{1,0:T(8,128)(2,1)}, bf16[64,2048]{1,0:T(8,128)(2,1)}, u32[]{:S(2)}, u32[]{:S(2)}) collective-permute-start(bf16[64,2048]{1,0:T(8,128)(2,1)} %fusion.109), channel_id=1, source_target_pairs={{0,1},{2,0},{4,2},{6,4},{7,6},{5,7},{3,5},{1,3},{8,10},{10,12},{12... | collective-permute-start | bytes 786440 | tf_op jit(solution)/shard_map/ppermute | solution.py:382
  1070.5 61.0 %collective-permute-start.256 = (bf16[128,9216]{1,0:T(8,128)(2,1)}, bf16[128,9216]{1,0:T(8,128)(2,1)S(1)}, u32[]{:S(2)}, u32[]{:S(2)}) collective-permute-start(bf16[128,9216]{1,0:T(8,128)(2,1)} %get-tuple-element.334), channel_id=1, source_target_pairs={{0,16},{16,0},{1,17},{17,1},{2,18},{18,2},{3,19},{19,3},{4,20},{20... | collective-permute-start | bytes 7077896 | tf_op jit(solution)/shard_map/ppermute | solution.py:368
  1122.0 44.8 %collective-permute-start.237 = (bf16[128,3072]{1,0:T(8,128)(2,1)}, bf16[128,3072]{1,0:T(8,128)(2,1)}, u32[]{:S(2)}, u32[]{:S(2)}) collective-permute-start(bf16[128,3072]{1,0:T(8,128)(2,1)} %get-tuple-element.309), channel_id=1, source_target_pairs={{0,16},{16,0},{1,17},{17,1},{2,18},{18,2},{3,19},{19,3},{4,20},{20... | collective-permute-start | bytes 2359304 | tf_op jit(solution)/shard_map/ppermute | solution.py:368
  (566 other events, 7130.8 us)

commit v4 on v3

--- a/solution.py
+++ b/solution.py
@@ -889,27 +889,24 @@
     section_out, _ = by_section(out_first, out_second)
     input_grads, facing = by_section(grad_first, grad_second)
 
-    def owned(name, widths, shared, token, other=None, skip=0):
-        firsts, seconds = back_first[name], back_second[other or name]
-        kept, sent = place_columns(firsts, seconds, flags, widths, shared, skip)
+    def owned(name, widths, shared, token):
+        firsts, seconds = back_first[name], back_second[name]
+        kept, sent = place_columns(firsts, seconds, flags, widths, shared, 0)
         taken = paired(sent, SECTION, 1)
         if token is not None:
             taken = gate(taken, token)
-        both = jnp.where(
-            plane == 0,
-            jnp.concatenate([kept, taken], axis=0),
-            jnp.concatenate([taken, kept], axis=0),
-        )
-        return both.astype(jnp.float32)
-
-    ff_total = w_gate.shape[2]
-    grad_mlp = owned("mlp", (ff_width,) * 3, (False,) * 3, None)
-    grad_attn = owned("attn", (head_size,) * 4, (False, True, True, False), facing)
-    edges = [0]
-    for array in (w_query, key_weight, value_weight, w_output):
-        edges.append(edges[-1] + array.shape[2])
-    attn_grads = [grad_attn[:, a:b] for a, b in zip(edges, edges[1:])]
-    mlp_grads = [grad_mlp[:, i * ff_total : (i + 1) * ff_total] for i in range(3)]
+        whole, left = [], 0
+        for width, wide in zip(widths, shared):
+            right = left + width * count // (2 if wide else 1)
+            mine, theirs = kept[:, left:right], taken[:, left:right]
+            halves_up = jnp.concatenate([mine, theirs], axis=0)
+            halves_down = jnp.concatenate([theirs, mine], axis=0)
+            whole.append(jnp.where(plane == 0, halves_up, halves_down).astype(jnp.float32))
+            left = right
+        return whole
+
+    mlp_grads = owned("mlp", (ff_width,) * 3, (False,) * 3, None)
+    attn_grads = owned("attn", (head_size,) * 4, (False, True, True, False), facing)
 
     rows_of = jnp.concatenate(
         [

time: 1180 us -> 1190 us (level)
    unnamed x669 -> x681, local copies, waits for them, and re-layouts: 27.1 us -> 24.6 us
where the time goes in v4:
time: 1190 us; the launch traced here: 1180 us
  waiting for transfers between devices  459 us (39%)
  starting transfers between devices  322 us (27%)
  matrix products  132 us (11%)
  other arithmetic  119 us (10%)
  Pallas kernels  82 us (7%)
  local copies, waits for them, and re-layouts  60.1 us (5%)
    ppermute x112, waiting for transfers between devices, ring(): return lax.ppermute(x, (TENSOR, DP), pairs)  235 us
    ppermute x150, waiting for transfers between devices, paired(): return lax.ppermute(x, axis, [(i, i ^ flip) for i in range(count)])  225 us
    ppermute x150, starting transfers between devices, paired(): return lax.ppermute(x, axis, [(i, i ^ flip) for i in range(count)])  199 us
    ppermute x112, starting transfers between devices, ring(): return lax.ppermute(x, (TENSOR, DP), pairs)  122 us
    dot_general x37, matrix products, dot_plain(): return jnp.dot(left, right, preferred_element_type=jnp.float32)  56.5 us
    dot_general x18, matrix products, dot_first(): lax.dot_general(left, right, (((0,), (0,)), ((), ())), preferred_element_...  42.7 us
    pallas_call x17, Pallas kernels, joined(): pl.pallas_call(kernel, out_shape=jax.ShapeDtypeStruct((rows, width), piec...  40.7 us
    dot_general x28, matrix products, dot_last(): lax.dot_general(left, right, (((1,), (1,)), ((), ())), preferred_element_...  32.5 us
  transfers between devices with their start and end apart: 262, of which 113 were waited for; matrix products, arithmetic and copies ran while one was open for 20% of the time, Pallas kernels for 6%

profile of v4, /device:TPU:0, one launch (start us, length us, event | category | flops | bytes accessed | tf_op | source)
XLA Modules:
  0.0 1178.8 jit_solution(15731744362666232961)
XLA Ops:
  61.4 6.6 collective-permute-start.30
  108.5 16.7 %collective-permute-done.34 = bf16[2048,128]{1,0:T(8,128)(2,1)} collective-permute-done((bf16[2048,128]{1,0:T(8,128)(2,1)S(1)}, bf16[2048,128]{1,0:T(8,128)(2,1)}, u32[]{:S(2)}, u32[]{:S(2)}) %collective-permute-start.34) | collective-permute-done | bytes 524320 | tf_op jit(solution)/shard_map/ppermute | solution.py:368
  158.2 7.5 collective-permute-done.37
  193.4 7.9 collective-permute-done.52.refs_2_
  209.9 8.6 collective-permute-done.55.refs_5_
  219.4 7.5 collective-permute-start.60
  245.6 12.0 %collective-permute-done.63.refs_5_ = bf16[256,384]{1,0:T(8,128)(2,1)S(1)} collective-permute-done((bf16[256,384]{1,0:T(8,128)(2,1)S(1)}, bf16[256,384]{1,0:T(8,128)(2,1)S(1)}, u32[]{:S(2)}, u32[]{:S(2)}) %collective-permute-start.63) | collective-permute-done | bytes 196640 | tf_op jit(solution)/shard_map/ppermute | solution.py:368
  260.8 7.2 collective-permute-start.72
  279.6 7.1 collective-permute-done.73.refs_3_
  296.0 10.6 collective-permute-done.75.refs_5_
  307.8 7.0 collective-permute-done.76.refs_6_
  364.4 24.5 %collective-permute-done.86 = bf16[2048,128]{1,0:T(8,128)(2,1)S(1)} collective-permute-done((bf16[2048,128]{1,0:T(8,128)(2,1)}, bf16[2048,128]{1,0:T(8,128)(2,1)S(1)}, u32[]{:S(2)}, u32[]{:S(2)}) %collective-permute-start.86) | collective-permute-done | bytes 524320 | tf_op jit(solution)/shard_map/ppermute | solution.py:368
  599.1 6.2 collective-permute-done.151
  618.9 6.2 collective-permute-done.156
  692.1 6.2 collective-permute-done.171
  810.7 17.6 %collective-permute-done.239.refs_1_ = bf16[1024,768]{1,0:T(8,128)(2,1)} collective-permute-done((bf16[1024,768]{1,0:T(8,128)(2,1)}, bf16[1024,768]{1,0:T(8,128)(2,1)}, u32[]{:S(2)}, u32[]{:S(2)}) %collective-permute-start.239) | collective-permute-done | bytes 1572896 | tf_op jit(solution)/shard_map/ppermute | solution.py:368
  839.4 5.8 collective-permute-done.195
  924.5 18.6 %collective-permute-done.245.refs_13_ = bf16[128,1152]{1,0:T(8,128)(2,1)} collective-permute-done((bf16[128,1152]{1,0:T(8,128)(2,1)}, bf16[128,1152]{1,0:T(8,128)(2,1)}, u32[]{:S(2)}, u32[]{:S(2)}) %collective-permute-start.245) | collective-permute-done | bytes 294944 | tf_op jit(solution)/shard_map/ppermute | solution.py:368
  943.1 12.7 %collective-permute-done.248.refs_3_ = bf16[1024,384]{1,0:T(8,128)(2,1)} collective-permute-done((bf16[1024,384]{1,0:T(8,128)(2,1)}, bf16[1024,384]{1,0:T(8,128)(2,1)}, u32[]{:S(2)}, u32[]{:S(2)}) %collective-permute-start.248) | collective-permute-done | bytes 786464 | tf_op jit(solution)/shard_map/ppermute | solution.py:368
  1003.0 7.7 collective-permute-done.226.refs_12_
  1024.8 10.6 collective-permute-done.211
  1041.1 17.9 %collective-permute-start.255 = (bf16[128,1152]{1,0:T(8,128)(2,1)}, bf16[128,1152]{1,0:T(8,128)(2,1)}, u32[]{:S(2)}, u32[]{:S(2)}) collective-permute-start(bf16[128,1152]{1,0:T(8,128)(2,1)} %get-tuple-element.332), channel_id=1, source_target_pairs={{0,7},{1,6},{2,5},{3,4},{4,3},{5,2},{6,1},{7,0},{8,15},{9,14},{10,... | collective-permute-start | bytes 884744 | tf_op jit(solution)/shard_map/ppermute | solution.py:368
  1077.6 9.4 collective-permute-start.231
  1138.6 7.9 collective-permute-start.257
  (1531 shorter events, 923.1 us)
Async XLA Ops:
  231.6 42.4 %collective-permute-start.40 = (bf16[64,2048]{1,0:T(8,128)(2,1)S(1)}, bf16[64,2048]{1,0:T(8,128)(2,1)S(1)}, u32[]{:S(2)}, u32[]{:S(2)}) collective-permute-start(bf16[64,2048]{1,0:T(8,128)(2,1)S(1)} %get-tuple-element.391), channel_id=1, source_target_pairs={{0,1},{2,0},{4,2},{6,4},{7,6},{5,7},{3,5},{1,3},{8,10},{10,12},{12... | collective-permute-start | bytes 786440 | tf_op jit(solution)/shard_map/ppermute | solution.py:382
  233.6 42.0 %collective-permute-start.44 = (bf16[64,2048]{1,0:T(8,128)(2,1)}, bf16[64,2048]{1,0:T(8,128)(2,1)}, u32[]{:S(2)}, u32[]{:S(2)}) collective-permute-start(bf16[64,2048]{1,0:T(8,128)(2,1)} %collective-permute-done.43), channel_id=1, source_target_pairs={{0,8},{8,0},{1,9},{9,1},{2,10},{10,2},{3,11},{11,3},{4,12},{12,4},... | collective-permute-start | bytes 786440 | tf_op jit(solution)/shard_map/ppermute | solution.py:368
  270.7 52.9 %collective-permute-start.58 = (bf16[2048,384]{1,0:T(8,128)(2,1)}, bf16[2048,384]{1,0:T(8,128)(2,1)}, u32[]{:S(2)}, u32[]{:S(2)}) collective-permute-start(bf16[2048,384]{1,0:T(8,128)(2,1)} %shard_map.243), channel_id=1, source_target_pairs={{0,16},{16,0},{1,17},{17,1},{2,18},{18,2},{3,19},{19,3},{4,20},{20... | collective-permute-start | bytes 4718600 | tf_op jit(solution)/shard_map/ppermute | solution.py:368
  274.1 65.6 %collective-permute-start.66 = (bf16[2048,384]{1,0:T(8,128)(2,1)}, bf16[2048,384]{1,0:T(8,128)(2,1)}, u32[]{:S(2)}, u32[]{:S(2)}) collective-permute-start(bf16[2048,384]{1,0:T(8,128)(2,1)} %shard_map.244), channel_id=1, source_target_pairs={{0,16},{16,0},{1,17},{17,1},{2,18},{18,2},{3,19},{19,3},{4,20},{20... | collective-permute-start | bytes 4718600 | tf_op jit(solution)/shard_map/ppermute | solution.py:368
  354.5 36.1 %collective-permute-start.78 = (bf16[2048,256]{1,0:T(8,128)(2,1)}, bf16[2048,256]{1,0:T(8,128)(2,1)}, u32[]{:S(2)}, u32[]{:S(2)}) collective-permute-start(bf16[2048,256]{1,0:T(8,128)(2,1)} %shard_map.246), channel_id=1, source_target_pairs={{0,16},{16,0},{1,17},{17,1},{2,18},{18,2},{3,19},{19,3},{4,20},{20... | collective-permute-start | bytes 3145736 | tf_op jit(solution)/shard_map/ppermute | solution.py:368
  355.0 38.7 %collective-permute-start.69 = (bf16[320,2048]{1,0:T(8,128)(2,1)}, bf16[320,2048]{1,0:T(8,128)(2,1)}, u32[]{:S(2)}, u32[]{:S(2)}) collective-permute-start(bf16[320,2048]{1,0:T(8,128)(2,1)} %shard_map.242), channel_id=1, source_target_pairs={{0,8},{8,0},{1,9},{9,1},{2,10},{10,2},{3,11},{11,3},{4,12},{12,4},... | collective-permute-start | bytes 3932168 | tf_op jit(solution)/shard_map/ppermute | solution.py:368
  769.2 41.5 %collective-permute-start.240 = (bf16[1024,384]{1,0:T(8,128)(2,1)}, bf16[1024,384]{1,0:T(8,128)(2,1)}, u32[]{:S(2)}, u32[]{:S(2)}) collective-permute-start(bf16[1024,384]{1,0:T(8,128)(2,1)} %get-tuple-element.438), channel_id=1, source_target_pairs={{0,16},{16,0},{1,17},{17,1},{2,18},{18,2},{3,19},{19,3},{4,20},{20... | collective-permute-start | bytes 2359304 | tf_op jit(solution)/shard_map/ppermute | solution.py:368
  790.7 37.6 %collective-permute-start.239 = (bf16[1024,768]{1,0:T(8,128)(2,1)}, bf16[1024,768]{1,0:T(8,128)(2,1)}, u32[]{:S(2)}, u32[]{:S(2)}) collective-permute-start(bf16[1024,768]{1,0:T(8,128)(2,1)} %get-tuple-element.413), channel_id=1, source_target_pairs={{0,16},{16,0},{1,17},{17,1},{2,18},{18,2},{3,19},{19,3},{4,20},{20... | collective-permute-start | bytes 4718600 | tf_op jit(solution)/shard_map/ppermute | solution.py:368
  797.2 39.3 %collective-permute-start.189 = (bf16[320,2048]{1,0:T(8,128)(2,1)}, bf16[320,2048]{1,0:T(8,128)(2,1)}, u32[]{:S(2)}, u32[]{:S(2)}) collective-permute-start(bf16[320,2048]{1,0:T(8,128)(2,1)} %convolution_convert_fusion.3), channel_id=1, source_target_pairs={{0,8},{8,0},{1,9},{9,1},{2,10},{10,2},{3,11},{11,3},{4,12},{12,4},... | collective-permute-start | bytes 3932168 | tf_op jit(solution)/shard_map/ppermute | solution.py:368
  802.7 67.1 %collective-permute-start.145 = (bf16[64,2048]{1,0:T(8,128)(2,1)}, bf16[64,2048]{1,0:T(8,128)(2,1)S(1)}, u32[]{:S(2)}, u32[]{:S(2)}) collective-permute-start(bf16[64,2048]{1,0:T(8,128)(2,1)} %select_n.912), channel_id=1, source_target_pairs={{0,16},{16,0},{1,17},{17,1},{2,18},{18,2},{3,19},{19,3},{4,20},{20... | collective-permute-start | bytes 786440 | tf_op jit(solution)/shard_map/ppermute | solution.py:368
  832.5 46.1 %collective-permute-start.241 = (bf16[128,1152]{1,0:T(8,128)(2,1)}, bf16[128,1152]{1,0:T(8,128)(2,1)S(1)}, u32[]{:S(2)}, u32[]{:S(2)}) collective-permute-start(bf16[128,1152]{1,0:T(8,128)(2,1)} %get-tuple-element.315), channel_id=1, source_target_pairs={{0,1},{1,0},{2,3},{3,2},{4,5},{5,4},{6,7},{7,6},{8,9},{9,8},{10,11... | collective-permute-start | bytes 884744 | tf_op jit(solution)/shard_map/ppermute | solution.py:368
  833.4 45.7 %collective-permute-start.242 = (bf16[128,1152]{1,0:T(8,128)(2,1)}, bf16[128,1152]{1,0:T(8,128)(2,1)S(1)}, u32[]{:S(2)}, u32[]{:S(2)}) collective-permute-start(bf16[128,1152]{1,0:T(8,128)(2,1)} %get-tuple-element.316), channel_id=1, source_target_pairs={{0,2},{1,3},{2,0},{3,1},{4,6},{5,7},{6,4},{7,5},{8,10},{9,11},{10,... | collective-permute-start | bytes 884744 | tf_op jit(solution)/shard_map/ppermute | solution.py:368
  880.5 76.8 %collective-permute-start.238 = (bf16[1024,768]{1,0:T(8,128)(2,1)}, bf16[1024,768]{1,0:T(8,128)(2,1)}, u32[]{:S(2)}, u32[]{:S(2)}) collective-permute-start(bf16[1024,768]{1,0:T(8,128)(2,1)} %get-tuple-element.415), channel_id=1, source_target_pairs={{0,16},{16,0},{1,17},{17,1},{2,18},{18,2},{3,19},{19,3},{4,20},{20... | collective-permute-start | bytes 4718600 | tf_op jit(solution)/shard_map/ppermute | solution.py:368
  894.9 60.9 %collective-permute-start.248 = (bf16[1024,384]{1,0:T(8,128)(2,1)}, bf16[1024,384]{1,0:T(8,128)(2,1)}, u32[]{:S(2)}, u32[]{:S(2)}) collective-permute-start(bf16[1024,384]{1,0:T(8,128)(2,1)} %get-tuple-element.436), channel_id=1, source_target_pairs={{0,16},{16,0},{1,17},{17,1},{2,18},{18,2},{3,19},{19,3},{4,20},{20... | collective-permute-start | bytes 2359304 | tf_op jit(solution)/shard_map/ppermute | solution.py:368
  906.2 36.8 %collective-permute-start.245 = (bf16[128,1152]{1,0:T(8,128)(2,1)}, bf16[128,1152]{1,0:T(8,128)(2,1)}, u32[]{:S(2)}, u32[]{:S(2)}) collective-permute-start(bf16[128,1152]{1,0:T(8,128)(2,1)} %get-tuple-element.319), channel_id=1, source_target_pairs={{0,5},{1,4},{2,7},{3,6},{4,1},{5,0},{6,3},{7,2},{8,13},{9,12},{10,... | collective-permute-start | bytes 884744 | tf_op jit(solution)/shard_map/ppermute | solution.py:368
  917.2 39.2 %collective-permute-start.246 = (bf16[128,1152]{1,0:T(8,128)(2,1)}, bf16[128,1152]{1,0:T(8,128)(2,1)S(1)}, u32[]{:S(2)}, u32[]{:S(2)}) collective-permute-start(bf16[128,1152]{1,0:T(8,128)(2,1)} %get-tuple-element.320), channel_id=1, source_target_pairs={{0,6},{1,7},{2,4},{3,5},{4,2},{5,3},{6,0},{7,1},{8,14},{9,15},{10,... | collective-permute-start | bytes 884744 | tf_op jit(solution)/shard_map/ppermute | solution.py:368
  918.4 38.5 %collective-permute-start.247 = (bf16[128,1152]{1,0:T(8,128)(2,1)}, bf16[128,1152]{1,0:T(8,128)(2,1)S(1)}, u32[]{:S(2)}, u32[]{:S(2)}) collective-permute-start(bf16[128,1152]{1,0:T(8,128)(2,1)} %get-tuple-element.321), channel_id=1, source_target_pairs={{0,7},{1,6},{2,5},{3,4},{4,3},{5,2},{6,1},{7,0},{8,15},{9,14},{10,... | collective-permute-start | bytes 884744 | tf_op jit(solution)/shard_map/ppermute | solution.py:368
  956.4 36.7 %collective-permute-start.146 = (bf16[2,64,2048]{2,1,0:T(8,128)(2,1)}, bf16[2,64,2048]{2,1,0:T(8,128)(2,1)}, u32[]{:S(2)}, u32[]{:S(2)}) collective-permute-start(bf16[2,64,2048]{2,1,0:T(8,128)(2,1)} %maximum_select_fusion.5), channel_id=1, source_target_pairs={{0,8},{8,0},{1,9},{9,1},{2,10},{10,2},{3,11},{11,3},{4,12},{12,4},... | collective-permute-start | bytes 1572872 | tf_op jit(solution)/shard_map/ppermute | solution.py:368
  956.9 38.7 %collective-permute-start.223 = (bf16[128,512]{1,0:T(8,128)(2,1)}, bf16[128,512]{1,0:T(8,128)(2,1)}, u32[]{:S(2)}, u32[]{:S(2)}) collective-permute-start(bf16[128,512]{1,0:T(8,128)(2,1)} %get-tuple-element.292), channel_id=1, source_target_pairs={{0,1},{1,0},{2,3},{3,2},{4,5},{5,4},{6,7},{7,6},{8,9},{9,8},{10,11... | collective-permute-start | bytes 393224 | tf_op jit(solution)/shard_map/ppermute | solution.py:368
  957.4 38.7 %collective-permute-start.224 = (bf16[128,512]{1,0:T(8,128)(2,1)}, bf16[128,512]{1,0:T(8,128)(2,1)}, u32[]{:S(2)}, u32[]{:S(2)}) collective-permute-start(bf16[128,512]{1,0:T(8,128)(2,1)} %get-tuple-element.293), channel_id=1, source_target_pairs={{0,2},{1,3},{2,0},{3,1},{4,6},{5,7},{6,4},{7,5},{8,10},{9,11},{10,... | collective-permute-start | bytes 393224 | tf_op jit(solution)/shard_map/ppermute | solution.py:368
  1000.9 58.0 %collective-permute-start.221 = (bf16[1024,512]{1,0:T(8,128)(2,1)}, bf16[1024,512]{1,0:T(8,128)(2,1)}, u32[]{:S(2)}, u32[]{:S(2)}) collective-permute-start(bf16[1024,512]{1,0:T(8,128)(2,1)} %get-tuple-element.430), channel_id=1, source_target_pairs={{0,16},{16,0},{1,17},{17,1},{2,18},{18,2},{3,19},{19,3},{4,20},{20... | collective-permute-start | bytes 3145736 | tf_op jit(solution)/shard_map/ppermute | solution.py:368
  1014.6 72.5 %collective-permute-start.209 = (bf16[320,2048]{1,0:T(8,128)(2,1)}, bf16[320,2048]{1,0:T(8,128)(2,1)S(1)}, u32[]{:S(2)}, u32[]{:S(2)}) collective-permute-start(bf16[320,2048]{1,0:T(8,128)(2,1)} %convolution_convert_fusion.2), channel_id=1, source_target_pairs={{0,8},{8,0},{1,9},{9,1},{2,10},{10,2},{3,11},{11,3},{4,12},{12,4},... | collective-permute-start | bytes 3932168 | tf_op jit(solution)/shard_map/ppermute | solution.py:368
  1076.3 54.4 %collective-permute-start.256 = (bf16[128,9216]{1,0:T(8,128)(2,1)}, bf16[128,9216]{1,0:T(8,128)(2,1)}, u32[]{:S(2)}, u32[]{:S(2)}) collective-permute-start(bf16[128,9216]{1,0:T(8,128)(2,1)} %get-tuple-element.334), channel_id=1, source_target_pairs={{0,16},{16,0},{1,17},{17,1},{2,18},{18,2},{3,19},{19,3},{4,20},{20... | collective-permute-start | bytes 7077896 | tf_op jit(solution)/shard_map/ppermute | solution.py:368
  1118.9 51.7 %collective-permute-start.237 = (bf16[128,3072]{1,0:T(8,128)(2,1)}, bf16[128,3072]{1,0:T(8,128)(2,1)}, u32[]{:S(2)}, u32[]{:S(2)}) collective-permute-start(bf16[128,3072]{1,0:T(8,128)(2,1)} %get-tuple-element.309), channel_id=1, source_target_pairs={{0,16},{16,0},{1,17},{17,1},{2,18},{18,2},{3,19},{19,3},{4,20},{20... | collective-permute-start | bytes 2359304 | tf_op jit(solution)/shard_map/ppermute | solution.py:368
  (572 other events, 7187.5 us)
